TPU v7x, 32 devices: a whole 2x2x4 slice. The times are simulated.
32 devices in a mesh: dp: 2 (over x), cluster: 16 (over z, y, core).
Axes of the slice: x: 2, y: 2, z: 4, core: 2. Of those that a mesh axis runs over, the one named last changes fastest.
Arguments:
- queries: bfloat16 [4096, 768], P(('dp', 'cluster')), may hold values from -6 to 6
- shortlist: int32 [4096, 8], P(('dp', 'cluster')), may hold values from 0 to 15, all different within a row; in each aligned block of 128 rows (0 to 127, 128 to 255, ...) at most 128 rows name the same one
- positives: int32 [4096, 8], P(('dp', 'cluster')), may hold values from 0 to 255
- weights: bfloat16 [16, 256, 768], P('cluster'), may hold values from -0.21875 to 0.21875
- first_moment: float32 [16, 256, 768], P('cluster'), may hold values from -24 to 24
- second_moment: float32 [16, 256, 768], P('cluster'), may hold values from 0.5 to 50
Outputs:
- new_weights: bfloat16 [16, 256, 768], P('cluster')
- new_first: float32 [16, 256, 768], P('cluster')
- new_second: float32 [16, 256, 768], P('cluster')
- query_grad: bfloat16 [4096, 768], P(('dp', 'cluster'))
Inputs may be any that keep to these rules, and one draw needn't show every extreme that they name: `shortlist`: each row names 8 different clusters. In the rows of one device no cluster is named by more than 128 rows, a bound that some block reaches of them.
All inputs are finite; a program needn't handle non-finite values.
Results may differ from a plain program's by a relative error of at most 0.0085.
Values may be sent and summed in bfloat16 or wider, within the bound.
No kernel may reach another device: no remote copies, remote signals or barrier semaphores. Data moves between devices by JAX's collectives and lax.ppermute only.
A program may use at most 64 MiB of HBM per device.

v0:
```python
import functools

import jax
import jax.numpy as jnp
from jax import lax
from jax.experimental import pallas as pl
from jax.experimental.pallas import tpu as pltpu
from jax.sharding import PartitionSpec as P


beta_one = 0.9
beta_two = 0.999
learn_rate = 0.01
adam_eps = 1e-08
adam_step = 10.0

NEAR = 4
KERNEL_VMEM = 16 << 20


def adam_update(cluster_weights, first_moment, second_moment, gradient):
    first_new = beta_one * first_moment + (1.0 - beta_one) * gradient
    second_new = beta_two * second_moment + (1.0 - beta_two) * gradient * gradient
    first_hat = first_new / (1.0 - beta_one**adam_step)
    second_hat = second_new / (1.0 - beta_two**adam_step)
    stepped = cluster_weights.astype(jnp.float32) - learn_rate * first_hat / (
        jnp.sqrt(second_hat) + adam_eps
    )
    return (stepped.astype(jnp.bfloat16), first_new, second_new)


def tn_dot(a, b):
    return lax.dot_general(a, b, (((0,), (0,)), ((), ())), preferred_element_type=jnp.float32)


def nt_dot(a, b):
    return lax.dot_general(a, b, (((1,), (1,)), ((), ())), preferred_element_type=jnp.float32)


def kernel_call(kernel, outs, args, flops):
    vmem = pl.BlockSpec(memory_space=pltpu.VMEM)
    specs = [pl.BlockSpec(memory_space=pltpu.SMEM)] + [vmem] * (len(args) - 1)
    return pl.pallas_call(
        kernel,
        out_shape=tuple(jax.ShapeDtypeStruct(shape, kind) for shape, kind in outs),
        in_specs=specs,
        out_specs=tuple([vmem] * len(outs)),
        compiler_params=pltpu.CompilerParams(vmem_limit_bytes=KERNEL_VMEM),
        cost_estimate=pl.CostEstimate(flops=flops, bytes_accessed=1 << 20, transcendentals=0),
    )(*args)


def coefficients(weights, q, listed, positive, cluster):
    labels, rows = weights.shape[0], q.shape[0]
    code = jnp.max(jnp.where(listed == cluster, positive, -1.0), axis=0, keepdims=True)
    label_ids = lax.broadcasted_iota(jnp.int32, (labels, rows), 0)
    target = (label_ids == code.astype(jnp.int32)).astype(jnp.float32)
    coef = jax.nn.sigmoid(nt_dot(weights, q)) - target
    return jnp.where(code >= 0.0, coef, 0.0).astype(jnp.bfloat16)


def unpack(packed_refs, rows, fanout):
    spare = [ref[rows : rows + fanout, :].astype(jnp.float32) for ref in packed_refs]
    q = jnp.concatenate([ref[:rows, :] for ref in packed_refs], axis=0)
    listed = jnp.concatenate([x[:, :rows] for x in spare], axis=1)
    positive = jnp.concatenate([x[:, rows : 2 * rows] for x in spare], axis=1)
    return q, listed, positive


def pack_kernel(base_ref, q_ref, listed_ref, positive_ref, out_ref):
    rows, dim = q_ref.shape
    fanout = listed_ref.shape[0]
    out_ref[:rows, :] = q_ref[...]
    ints = [listed_ref[...], positive_ref[...]]
    if dim > 2 * rows:
        ints.append(jnp.zeros((fanout, dim - 2 * rows), jnp.int32))
    spare = jnp.concatenate(ints, axis=1)
    out_ref[rows:, :] = spare.astype(jnp.float32).astype(jnp.bfloat16)


def own_kernel(rows, base_ref, packed_ref, *refs):
    weight_refs, (out_ref, coef_ref) = refs[:NEAR], refs[NEAR:]
    labels = weight_refs[0].shape[0]
    q, listed, positive = unpack([packed_ref], rows, packed_ref.shape[0] - rows)
    total = jnp.zeros(out_ref.shape, jnp.float32)
    for j in range(NEAR):
        w = weight_refs[j][...]
        cluster = jnp.bitwise_xor(base_ref[0], j).astype(jnp.float32)
        coef = coefficients(w, q, listed, positive, cluster)
        coef_ref[j * labels : (j + 1) * labels, :] = coef
        total = total + tn_dot(coef, w)
    out_ref[...] = total


def grad_kernel(rows, base_ref, own_coef_ref, *refs):
    packed_refs, weight_refs = refs[:NEAR], refs[NEAR : 2 * NEAR]
    coef_ref, send_ref, own_ref, beside_ref = refs[2 * NEAR :]
    labels = weight_refs[0].shape[0]
    fanout = packed_refs[0].shape[0] - rows
    q, listed, positive = unpack(packed_refs[1:], rows, fanout)
    own_q = packed_refs[0][:rows, :]

    def part(j):
        cluster = jnp.bitwise_xor(base_ref[0], j).astype(jnp.float32)
        coef = coefficients(weight_refs[j][...], q, listed, positive, cluster)
        spot = slice(j * labels, (j + 1) * labels)
        coef_ref[spot, :] = coef
        return jnp.dot(coef, q, preferred_element_type=jnp.float32) + jnp.dot(
            own_coef_ref[spot, :], own_q, preferred_element_type=jnp.float32
        )

    send_ref[:labels, :] = part(1).astype(jnp.bfloat16)
    send_ref[labels:, :] = part(3).astype(jnp.bfloat16)
    own_ref[...] = part(0)
    beside_ref[...] = part(2)


def back_kernel(rows, base_ref, coef_ref, *refs):
    weight_refs, out_refs = refs[:NEAR], refs[NEAR:]
    labels = weight_refs[0].shape[0]
    total = jnp.zeros((coef_ref.shape[1], weight_refs[0].shape[1]), jnp.float32)
    for j in range(NEAR):
        total = total + tn_dot(coef_ref[j * labels : (j + 1) * labels, :], weight_refs[j][...])
    for s, out_ref in enumerate(out_refs):
        out_ref[...] = total[s * rows : (s + 1) * rows, :].astype(jnp.bfloat16)


def near_device(queries, shortlist, positives, weights, first_moment, second_moment):
    owners = lax.axis_size("cluster")
    lines = owners // NEAR
    rows, fanout = shortlist.shape
    labels, dim = weights.shape[1:]
    half = labels // 2
    others = (lines - 1) * rows
    base = lax.axis_index("cluster").astype(jnp.int32).reshape(1)
    low_type, wide = jnp.bfloat16, jnp.float32

    def over_cluster(x, bits):
        return lax.ppermute(x, "cluster", [(i, i ^ bits) for i in range(owners)])

    def over_dp(x):
        return lax.ppermute(x, "dp", [(0, 1), (1, 0)])

    own_weights = weights[0]
    (packed,) = kernel_call(
        pack_kernel,
        [((rows + fanout, dim), low_type)],
        [base, queries, shortlist.T, positives.T],
        0,
    )
    packs = [packed] + [over_cluster(packed, NEAR * s) for s in range(1, lines)]
    weight_core = over_cluster(own_weights, 1)
    beside = over_cluster(own_weights, 2)
    near_weights = [own_weights, weight_core, beside, over_cluster(beside, 1)]

    total, own_coef = kernel_call(
        functools.partial(own_kernel, rows),
        [((rows, dim), wide), ((NEAR * labels, rows), low_type)],
        [base, packed, *near_weights],
        4 * rows * NEAR * labels * dim,
    )
    coef, send, own, near = kernel_call(
        functools.partial(grad_kernel, rows),
        [
            ((NEAR * labels, others), low_type),
            ((2 * labels, dim), low_type),
            ((labels, dim), wide),
            ((labels, dim), wide),
        ],
        [base, own_coef, *packs, *near_weights],
        4 * others * NEAR * labels * dim,
    )
    got = over_cluster(send, 1).astype(wide)
    backs = kernel_call(
        functools.partial(back_kernel, rows),
        [((rows, dim), low_type)] * (lines - 1),
        [base, coef, *near_weights],
        2 * others * NEAR * labels * dim,
    )
    for s in range(1, lines):
        total = total + over_cluster(backs[s - 1], NEAR * s).astype(wide)
    query_grad = total.astype(low_type)

    own = own + got[:labels]
    near = near + got[labels:]
    low = jnp.concatenate([own[half:], near[half:]], axis=0).astype(low_type)
    got_top = over_cluster(near[:half].astype(low_type), 2).astype(wide)
    got_low = over_dp(low).astype(wide)
    top = (own[:half] + got_top).astype(low_type)
    low = low.astype(wide) + got_low
    top = top.astype(wide) + over_dp(top).astype(wide)
    low_own = low[:half] + over_cluster(low[half:].astype(low_type), 2).astype(wide)
    gradient = jnp.concatenate([top, low_own], axis=0)
    new_weights, new_first, new_second = adam_update(
        own_weights, first_moment[0], second_moment[0], gradient
    )
    return (new_weights[None], new_first[None], new_second[None], query_grad)


def owner_work(arrived_rows, arrived_labels, cluster_rows):
    label_ids = jnp.arange(cluster_rows.shape[0], dtype=jnp.int32)
    scores = lax.dot_general(
        arrived_rows, cluster_rows, (((1,), (1,)), ((), ())), preferred_element_type=jnp.float32
    )
    target = (arrived_labels[:, None] == label_ids[None, :]).astype(jnp.float32)
    coefficient = (jax.nn.sigmoid(scores) - target).astype(jnp.bfloat16)
    gradient = lax.dot_general(
        coefficient, arrived_rows, (((0,), (0,)), ((), ())), preferred_element_type=jnp.float32
    )
    visit_grad = jnp.dot(coefficient, cluster_rows, preferred_element_type=jnp.float32).astype(
        jnp.bfloat16
    )
    return (gradient, visit_grad)


def dispatch_device(queries, shortlist, positives, weights, first_moment, second_moment):
    owners = lax.axis_size("cluster")
    rows_dev, fanout = shortlist.shape
    feature_dim = queries.shape[1]
    capacity = min(rows_dev, 2 * rows_dev * fanout // owners)
    visits = shortlist.reshape(-1)
    labels = positives.reshape(-1)
    onehot = (visits[:, None] == jnp.arange(owners, dtype=jnp.int32)[None, :]).astype(jnp.int32)
    visit_rank = jnp.sum((jnp.cumsum(onehot, axis=0) - onehot) * onehot, axis=1)
    slot_index = visits * capacity + visit_rank
    slot_visit = (
        jnp.full((owners * capacity,), -1, jnp.int32)
        .at[slot_index]
        .set(jnp.arange(visits.shape[0], dtype=jnp.int32))
    )
    filled = slot_visit >= 0
    clamped = jnp.maximum(slot_visit, 0)
    send_rows = jnp.where(filled[:, None], queries[clamped // fanout], jnp.zeros((), queries.dtype))
    send_labels = jnp.where(filled, labels[clamped], -1)
    cluster_rows = weights[0]
    exchange = functools.partial(
        lax.all_to_all, axis_name="cluster", split_axis=0, concat_axis=0, tiled=True
    )
    arrived_rows = exchange(send_rows.reshape(owners, capacity, feature_dim))
    arrived_labels = exchange(send_labels.reshape(owners, capacity))
    gradient, visit_grad = owner_work(
        arrived_rows.reshape(-1, feature_dim), arrived_labels.reshape(-1), cluster_rows
    )
    returned = exchange(visit_grad.reshape(owners, capacity, feature_dim))
    per_visit = returned.reshape(-1, feature_dim)[slot_index].astype(jnp.float32)
    query_grad = jnp.sum(per_visit.reshape(rows_dev, fanout, feature_dim), axis=1).astype(
        jnp.bfloat16
    )
    summed = lax.psum(gradient.astype(jnp.bfloat16), "dp").astype(jnp.float32)
    new_weights, new_first, new_second = adam_update(
        cluster_rows, first_moment[0], second_moment[0], summed
    )
    return (new_weights[None], new_first[None], new_second[None], query_grad)


def on_device(queries, shortlist, *rest):
    owners, copies = lax.axis_size("cluster"), lax.axis_size("dp")
    rows_dev, fanout = shortlist.shape
    dense = 2 * fanout >= owners and owners == NEAR * NEAR and copies == 2
    dense = dense and rest[1].shape[1] <= 256 and queries.shape[1] >= 2 * rows_dev
    step = near_device if dense else dispatch_device
    return step(queries, shortlist, *rest)


def solution(mesh):
    split = P(("dp", "cluster"), None)
    owned = P("cluster", None, None)
    return jax.shard_map(
        on_device,
        mesh=mesh,
        in_specs=(split, split, split, owned, owned, owned),
        out_specs=(owned, owned, owned, split),
        check_vma=False,
    )
```

profile of v0, /device:TPU:8, one launch (start us, length us, event | category | flops | bytes accessed | tf_op | source)
XLA Modules:
  0.0 70.2 jit_solution(4350810285804523949)
XLA Ops:
  0.6 1.6 %collective-permute-start.1 = (bf16[256,768]{1,0:T(8,128)(2,1)}, bf16[256,768]{1,0:T(8,128)(2,1)S(1)}, u32[]{:S(2)}, u32[]{:S(2)}) collective-permute-start(bf16[256,768]{1,0:T(8,128)(2,1)} %bitcast.8), channel_id=1, source_target_pairs={{0,2},{1,3},{2,0},{3,1},{4,6},{5,7},{6,4},{7,5},{8,10},{9,11},{10,... | collective-permute-start | bytes 1179656 | tf_op jit(solution)/shard_map/ppermute | solution.py:139
  2.2 0.0 collective-permute-start
  2.2 9.5 %collective-permute-done.1.refs_2_.refs_6_ = bf16[256,768]{1,0:T(8,128)(2,1)S(1)} collective-permute-done((bf16[256,768]{1,0:T(8,128)(2,1)}, bf16[256,768]{1,0:T(8,128)(2,1)S(1)}, u32[]{:S(2)}, u32[]{:S(2)}) %collective-permute-start.1) | collective-permute-done | bytes 393248 | tf_op jit(solution)/shard_map/ppermute | solution.py:139
  11.8 0.0 collective-permute-start.2
  11.8 0.0 copy-start.2
  11.8 0.9 %copy-done.2 = bf16[128,768]{1,0:T(8,128)(2,1)S(1)} copy-done((bf16[128,768]{1,0:T(8,128)(2,1)S(1)}, bf16[128,768]{1,0:T(8,128)(2,1)}, u32[]{:S(2)}) %copy-start.2) | copy-done | bytes 196632
  12.7 0.0 copy-start.3
  12.7 0.7 copy-done.3
  13.4 0.0 copy-start.4
  13.4 0.7 copy-done.4
  14.1 1.6 %collective-permute-start.5 = (bf16[136,768]{1,0:T(8,128)(2,1)S(1)}, bf16[136,768]{1,0:T(8,128)(2,1)S(1)}, u32[]{:S(2)}, u32[]{:S(2)}) collective-permute-start(bf16[136,768]{1,0:T(8,128)(2,1)S(1)} %shard_map.93.packed_ref.refs_0_), channel_id=1, source_target_pairs={{0,12},{1,13},{2,14},{3,15},{4,8},{5,9},{6,10},{7,11},{8,4},{9,5},... | collective-permute-start | bytes 626696 | tf_op jit(solution)/shard_map/ppermute | solution.py:139
  15.7 1.1 %collective-permute-start.4 = (bf16[136,768]{1,0:T(8,128)(2,1)S(1)}, bf16[136,768]{1,0:T(8,128)(2,1)S(1)}, u32[]{:S(2)}, u32[]{:S(2)}) collective-permute-start(bf16[136,768]{1,0:T(8,128)(2,1)S(1)} %shard_map.93.packed_ref.refs_0_), channel_id=1, source_target_pairs={{0,8},{1,9},{2,10},{3,11},{4,12},{5,13},{6,14},{7,15},{8,0},{9,1},... | collective-permute-start | bytes 626696 | tf_op jit(solution)/shard_map/ppermute | solution.py:139
  16.8 1.4 %collective-permute-start.3 = (bf16[136,768]{1,0:T(8,128)(2,1)S(1)}, bf16[136,768]{1,0:T(8,128)(2,1)S(1)}, u32[]{:S(2)}, u32[]{:S(2)}) collective-permute-start(bf16[136,768]{1,0:T(8,128)(2,1)S(1)} %shard_map.93.packed_ref.refs_0_), channel_id=1, source_target_pairs={{0,4},{1,5},{2,6},{3,7},{4,0},{5,1},{6,2},{7,3},{8,12},{9,13},{10,... | collective-permute-start | bytes 626696 | tf_op jit(solution)/shard_map/ppermute | solution.py:139
  18.2 0.0 collective-permute-done.refs_1_.refs_5_
  18.2 0.0 collective-permute-done.2.refs_3_.refs_7_
  18.2 0.0 copy-start
  18.2 1.0 %copy-done = bf16[1,256,768]{2,1,0:T(8,128)(2,1)S(1)} copy-done((bf16[1,256,768]{2,1,0:T(8,128)(2,1)S(1)}, bf16[1,256,768]{2,1,0:T(8,128)(2,1)}, u32[]{:S(2)}) %copy-start) | copy-done | bytes 393240
  19.2 1.6 %shard_map.94 = (f32[128,768]{1,0:T(8,128)S(1)}, bf16[1024,128]{1,0:T(8,128)(2,1)S(1)}) custom-call(s32[1]{0:T(128)} %bitcast.base_ref, bf16[136,768]{1,0:T(8,128)(2,1)S(1)} %shard_map.93.packed_ref.refs_0_, bf16[256,768]{1,0:T(8,128)(2,1)S(1)} %bitcast.10, bf16[256,768]{1,0:T(8,128)(2,1)S(1)} %collective-permute-done.refs_1_.refs_5_, ...), custom_call_target="tpu_custom_call" | custom-call | flops 402653184 | bytes 1048576 | tf_op jit(solution)/shard_map/pallas_call | solution.py:43
  20.8 10.3 %collective-permute-done.5.refs_3_ = bf16[136,768]{1,0:T(8,128)(2,1)S(1)} collective-permute-done((bf16[136,768]{1,0:T(8,128)(2,1)S(1)}, bf16[136,768]{1,0:T(8,128)(2,1)S(1)}, u32[]{:S(2)}, u32[]{:S(2)}) %collective-permute-start.5) | collective-permute-done | bytes 208928 | tf_op jit(solution)/shard_map/ppermute | solution.py:139
  31.1 3.1 %collective-permute-done.4.refs_2_ = bf16[136,768]{1,0:T(8,128)(2,1)S(1)} collective-permute-done((bf16[136,768]{1,0:T(8,128)(2,1)S(1)}, bf16[136,768]{1,0:T(8,128)(2,1)S(1)}, u32[]{:S(2)}, u32[]{:S(2)}) %collective-permute-start.4) | collective-permute-done | bytes 208928 | tf_op jit(solution)/shard_map/ppermute | solution.py:139
  34.3 0.0 collective-permute-done.3.refs_1_
  34.3 0.0 copy-start.1
  34.3 2.6 %shard_map.95 = (bf16[1024,384]{1,0:T(8,128)(2,1)S(1)}, bf16[512,768]{1,0:T(8,128)(2,1)S(1)}, f32[256,768]{1,0:T(8,128)S(1)}, f32[256,768]{1,0:T(8,128)S(1)}) custom-call(s32[1]{0:T(128)} %bitcast.base_ref, bf16[1024,128]{1,0:T(8,128)(2,1)S(1)} %get-tuple-element.13.own_coef_ref, bf16[136,768]{1,0:T(8,128)(2,1)S(1)} %shard_map.93.packed_ref.refs_0_, ...), custom_call_target="tpu_custom_call" | custom-call | flops 1207959552 | bytes 1048576 | tf_op jit(solution)/shard_map/pallas_call | solution.py:43
  36.9 0.1 collective-permute-start.6
  37.0 0.0 copy-done.1
  37.0 0.8 %shard_map.96 = (bf16[128,768]{1,0:T(8,128)(2,1)S(1)}, bf16[128,768]{1,0:T(8,128)(2,1)S(1)}, bf16[128,768]{1,0:T(8,128)(2,1)S(1)}) custom-call(s32[1]{0:T(128)} %bitcast.base_ref, bf16[1024,384]{1,0:T(8,128)(2,1)S(1)} %get-tuple-element.18.coef_ref, bf16[256,768]{1,0:T(8,128)(2,1)S(1)} %bitcast.12, ...), custom_call_target="tpu_custom_call" | custom-call | flops 603979776 | bytes 1048576 | tf_op jit(solution)/shard_map/pallas_call | solution.py:43
  37.8 2.4 %collective-permute-start.11 = (bf16[128,768]{1,0:T(8,128)(2,1)S(1)}, bf16[128,768]{1,0:T(8,128)(2,1)S(1)}, u32[]{:S(2)}, u32[]{:S(2)}) collective-permute-start(bf16[128,768]{1,0:T(8,128)(2,1)S(1)} %get-tuple-element.19), channel_id=1, source_target_pairs={{0,4},{1,5},{2,6},{3,7},{4,0},{5,1},{6,2},{7,3},{8,12},{9,13},{10,... | collective-permute-start | bytes 589832 | tf_op jit(solution)/shard_map/ppermute | solution.py:139
  40.2 1.1 %collective-permute-start.12 = (bf16[128,768]{1,0:T(8,128)(2,1)S(1)}, bf16[128,768]{1,0:T(8,128)(2,1)S(1)}, u32[]{:S(2)}, u32[]{:S(2)}) collective-permute-start(bf16[128,768]{1,0:T(8,128)(2,1)S(1)} %get-tuple-element.20), channel_id=1, source_target_pairs={{0,8},{1,9},{2,10},{3,11},{4,12},{5,13},{6,14},{7,15},{8,0},{9,1},... | collective-permute-start | bytes 589832 | tf_op jit(solution)/shard_map/ppermute | solution.py:139
  41.3 0.5 collective-permute-start.13
  41.8 0.0 collective-permute-done.6
  41.8 0.1 convert_element_type.48
  41.9 0.2 slice_add_fusion.1
  42.2 1.6 %collective-permute-start.7 = (bf16[128,768]{1,0:T(8,128)(2,1)S(1)}, bf16[128,768]{1,0:T(8,128)(2,1)S(1)}, u32[]{:S(2)}, u32[]{:S(2)}) collective-permute-start(bf16[128,768]{1,0:T(8,128)(2,1)S(1)} %get-tuple-element.27), channel_id=1, source_target_pairs={{0,2},{1,3},{2,0},{3,1},{4,6},{5,7},{6,4},{7,5},{8,10},{9,11},{10,... | collective-permute-start | bytes 589832 | tf_op jit(solution)/shard_map/ppermute | solution.py:139
  43.8 1.6 %collective-permute-start.9 = (bf16[256,768]{1,0:T(8,128)(2,1)S(1)}, bf16[256,768]{1,0:T(8,128)(2,1)S(1)}, u32[]{:S(2)}, u32[]{:S(2)}) collective-permute-start(bf16[256,768]{1,0:T(8,128)(2,1)S(1)} %pad_maximum_fusion.1), channel_id=1, source_target_pairs={{0,16},{16,0},{1,17},{17,1},{2,18},{18,2},{3,19},{19,3},{4,20},{20... | collective-permute-start | bytes 1179656 | tf_op jit(solution)/shard_map/ppermute | solution.py:142
  45.4 3.5 %collective-permute-done.11 = bf16[128,768]{1,0:T(8,128)(2,1)S(1)} collective-permute-done((bf16[128,768]{1,0:T(8,128)(2,1)S(1)}, bf16[128,768]{1,0:T(8,128)(2,1)S(1)}, u32[]{:S(2)}, u32[]{:S(2)}) %collective-permute-start.11) | collective-permute-done | bytes 196640 | tf_op jit(solution)/shard_map/ppermute | solution.py:139
  48.9 6.2 %collective-permute-done.12 = bf16[128,768]{1,0:T(8,128)(2,1)S(1)} collective-permute-done((bf16[128,768]{1,0:T(8,128)(2,1)S(1)}, bf16[128,768]{1,0:T(8,128)(2,1)S(1)}, u32[]{:S(2)}, u32[]{:S(2)}) %collective-permute-start.12) | collective-permute-done | bytes 196640 | tf_op jit(solution)/shard_map/ppermute | solution.py:139
  55.1 4.7 %collective-permute-done.13 = bf16[128,768]{1,0:T(8,128)(2,1)S(1)} collective-permute-done((bf16[128,768]{1,0:T(8,128)(2,1)S(1)}, bf16[128,768]{1,0:T(8,128)(2,1)S(1)}, u32[]{:S(2)}, u32[]{:S(2)}) %collective-permute-start.13) | collective-permute-done | bytes 196640 | tf_op jit(solution)/shard_map/ppermute | solution.py:139
  59.8 0.8 %add_convert_fusion = bf16[128,768]{1,0:T(8,128)(2,1)} fusion(bf16[128,768]{1,0:T(8,128)(2,1)S(1)} %collective-permute-done.13, bf16[128,768]{1,0:T(8,128)(2,1)S(1)} %collective-permute-done.12, f32[128,768]{1,0:T(8,128)S(1)} %get-tuple-element.17, bf16[128,768]{1,0:T(8,128)(2,1)S(1)} %collective-permute-done.11), kind=kLoop, calls=%fused_computation.16 | loop fusion | flops 688128 | bytes 1179648 | tf_op jit(solution)/shard_map/convert_element_type | solution.py:182
  60.5 0.0 collective-permute-done.7
  60.6 0.0 copy-start.5
  60.6 0.0 copy-start.6
  60.6 1.6 %collective-permute-start.8 = (bf16[128,768]{1,0:T(8,128)(2,1)S(1)}, bf16[128,768]{1,0:T(8,128)(2,1)S(1)}, u32[]{:S(2)}, u32[]{:S(2)}) collective-permute-start(bf16[128,768]{1,0:T(8,128)(2,1)S(1)} %fusion.3), channel_id=1, source_target_pairs={{0,16},{16,0},{1,17},{17,1},{2,18},{18,2},{3,19},{19,3},{4,20},{20... | collective-permute-start | bytes 589832 | tf_op jit(solution)/shard_map/ppermute | solution.py:142
  62.2 0.0 collective-permute-done.9
  62.2 0.1 convert_add_fusion
  62.3 1.6 %collective-permute-start.10 = (bf16[128,768]{1,0:T(8,128)(2,1)S(1)}, bf16[128,768]{1,0:T(8,128)(2,1)S(1)}, u32[]{:S(2)}, u32[]{:S(2)}) collective-permute-start(bf16[128,768]{1,0:T(8,128)(2,1)S(1)} %slice.56), channel_id=1, source_target_pairs={{0,2},{1,3},{2,0},{3,1},{4,6},{5,7},{6,4},{7,5},{8,10},{9,11},{10,... | collective-permute-start | bytes 589832 | tf_op jit(solution)/shard_map/ppermute | solution.py:139
  63.9 3.2 %collective-permute-done.8 = bf16[128,768]{1,0:T(8,128)(2,1)S(1)} collective-permute-done((bf16[128,768]{1,0:T(8,128)(2,1)S(1)}, bf16[128,768]{1,0:T(8,128)(2,1)S(1)}, u32[]{:S(2)}, u32[]{:S(2)}) %collective-permute-start.8) | collective-permute-done | bytes 196640 | tf_op jit(solution)/shard_map/ppermute | solution.py:142
  67.2 1.4 %collective-permute-done.10 = bf16[128,768]{1,0:T(8,128)(2,1)S(1)} collective-permute-done((bf16[128,768]{1,0:T(8,128)(2,1)S(1)}, bf16[128,768]{1,0:T(8,128)(2,1)S(1)}, u32[]{:S(2)}, u32[]{:S(2)}) %collective-permute-start.10) | collective-permute-done | bytes 196640 | tf_op jit(solution)/shard_map/ppermute | solution.py:139
  68.6 0.0 copy-done.5
  68.6 0.0 copy-done.6
  68.6 1.6 %subtract_convert_fusion = (bf16[1,256,768]{2,1,0:T(8,128)(2,1)}, f32[1,256,768]{2,1,0:T(8,128)}, f32[1,256,768]{2,1,0:T(8,128)}) fusion(bf16[1,256,768]{2,1,0:T(8,128)(2,1)S(1)} %copy-done.1, f32[1,128,768]{2,1,0:T(8,128)S(1)} %fusion.2, f32[1,128,768]{2,1,0:T(8,128)S(1)} %add_bitcast_fusion, f32[1,256,768]{2,1,0:T(8,128)S(1)} %copy-done.5, ...), kind=kLoop, calls=%fused_computation.6 | loop fusion | flops 2949120 | bytes 4718592 | tf_op jit(solution)/shard_map/convert_element_type | solution.py:29
  (8 shorter events, 0.2 us)
Async XLA Ops:
  0.6 11.1 %collective-permute-start.1 = (bf16[256,768]{1,0:T(8,128)(2,1)}, bf16[256,768]{1,0:T(8,128)(2,1)S(1)}, u32[]{:S(2)}, u32[]{:S(2)}) collective-permute-start(bf16[256,768]{1,0:T(8,128)(2,1)} %bitcast.8), channel_id=1, source_target_pairs={{0,2},{1,3},{2,0},{3,1},{4,6},{5,7},{6,4},{7,5},{8,10},{9,11},{10,... | collective-permute-start | bytes 1179656 | tf_op jit(solution)/shard_map/ppermute | solution.py:139
  2.2 16.0 %collective-permute-start = (bf16[256,768]{1,0:T(8,128)(2,1)}, bf16[256,768]{1,0:T(8,128)(2,1)S(1)}, u32[]{:S(2)}, u32[]{:S(2)}) collective-permute-start(bf16[256,768]{1,0:T(8,128)(2,1)} %bitcast.9), channel_id=1, source_target_pairs={{0,1},{1,0},{2,3},{3,2},{4,5},{5,4},{6,7},{7,6},{8,9},{9,8},{10,11... | collective-permute-start | bytes 1179656 | tf_op jit(solution)/shard_map/ppermute | solution.py:139
  11.8 6.5 %collective-permute-start.2 = (bf16[256,768]{1,0:T(8,128)(2,1)S(1)}, bf16[256,768]{1,0:T(8,128)(2,1)S(1)}, u32[]{:S(2)}, u32[]{:S(2)}) collective-permute-start(bf16[256,768]{1,0:T(8,128)(2,1)S(1)} %collective-permute-done.1.refs_2_.refs_6_), channel_id=1, source_target_pairs={{0,1},{1,0},{2,3},{3,2},{4,5},{5,4},{6,7},{7,6},{8,9},{9,8},{10,11... | collective-permute-start | bytes 1179656 | tf_op jit(solution)/shard_map/ppermute | solution.py:139
  11.8 0.9 %copy-start.2 = (bf16[128,768]{1,0:T(8,128)(2,1)S(1)}, bf16[128,768]{1,0:T(8,128)(2,1)}, u32[]{:S(2)}) copy-start(bf16[128,768]{1,0:T(8,128)(2,1)} %q_ref.1) | copy-start | bytes 589828
  12.7 0.7 copy-start.3
  13.4 0.7 copy-start.4
  14.1 17.1 %collective-permute-start.5 = (bf16[136,768]{1,0:T(8,128)(2,1)S(1)}, bf16[136,768]{1,0:T(8,128)(2,1)S(1)}, u32[]{:S(2)}, u32[]{:S(2)}) collective-permute-start(bf16[136,768]{1,0:T(8,128)(2,1)S(1)} %shard_map.93.packed_ref.refs_0_), channel_id=1, source_target_pairs={{0,12},{1,13},{2,14},{3,15},{4,8},{5,9},{6,10},{7,11},{8,4},{9,5},... | collective-permute-start | bytes 626696 | tf_op jit(solution)/shard_map/ppermute | solution.py:139
  15.7 18.5 %collective-permute-start.4 = (bf16[136,768]{1,0:T(8,128)(2,1)S(1)}, bf16[136,768]{1,0:T(8,128)(2,1)S(1)}, u32[]{:S(2)}, u32[]{:S(2)}) collective-permute-start(bf16[136,768]{1,0:T(8,128)(2,1)S(1)} %shard_map.93.packed_ref.refs_0_), channel_id=1, source_target_pairs={{0,8},{1,9},{2,10},{3,11},{4,12},{5,13},{6,14},{7,15},{8,0},{9,1},... | collective-permute-start | bytes 626696 | tf_op jit(solution)/shard_map/ppermute | solution.py:139
  16.8 17.4 %collective-permute-start.3 = (bf16[136,768]{1,0:T(8,128)(2,1)S(1)}, bf16[136,768]{1,0:T(8,128)(2,1)S(1)}, u32[]{:S(2)}, u32[]{:S(2)}) collective-permute-start(bf16[136,768]{1,0:T(8,128)(2,1)S(1)} %shard_map.93.packed_ref.refs_0_), channel_id=1, source_target_pairs={{0,4},{1,5},{2,6},{3,7},{4,0},{5,1},{6,2},{7,3},{8,12},{9,13},{10,... | collective-permute-start | bytes 626696 | tf_op jit(solution)/shard_map/ppermute | solution.py:139
  18.2 1.0 %copy-start = (bf16[1,256,768]{2,1,0:T(8,128)(2,1)S(1)}, bf16[1,256,768]{2,1,0:T(8,128)(2,1)}, u32[]{:S(2)}) copy-start(bf16[1,256,768]{2,1,0:T(8,128)(2,1)} %param.9) | copy-start | bytes 1179652
  34.3 2.7 %copy-start.1 = (bf16[1,256,768]{2,1,0:T(8,128)(2,1)S(1)}, bf16[1,256,768]{2,1,0:T(8,128)(2,1)}, u32[]{:S(2)}) copy-start(bf16[1,256,768]{2,1,0:T(8,128)(2,1)} %param.9) | copy-start | bytes 1179652
  36.9 4.9 %collective-permute-start.6 = (bf16[512,768]{1,0:T(8,128)(2,1)S(1)}, bf16[512,768]{1,0:T(8,128)(2,1)S(1)}, u32[]{:S(2)}, u32[]{:S(2)}) collective-permute-start(bf16[512,768]{1,0:T(8,128)(2,1)S(1)} %get-tuple-element.15), channel_id=1, source_target_pairs={{0,1},{1,0},{2,3},{3,2},{4,5},{5,4},{6,7},{7,6},{8,9},{9,8},{10,11... | collective-permute-start | bytes 2359304 | tf_op jit(solution)/shard_map/ppermute | solution.py:139
  37.8 11.1 %collective-permute-start.11 = (bf16[128,768]{1,0:T(8,128)(2,1)S(1)}, bf16[128,768]{1,0:T(8,128)(2,1)S(1)}, u32[]{:S(2)}, u32[]{:S(2)}) collective-permute-start(bf16[128,768]{1,0:T(8,128)(2,1)S(1)} %get-tuple-element.19), channel_id=1, source_target_pairs={{0,4},{1,5},{2,6},{3,7},{4,0},{5,1},{6,2},{7,3},{8,12},{9,13},{10,... | collective-permute-start | bytes 589832 | tf_op jit(solution)/shard_map/ppermute | solution.py:139
  40.2 14.9 %collective-permute-start.12 = (bf16[128,768]{1,0:T(8,128)(2,1)S(1)}, bf16[128,768]{1,0:T(8,128)(2,1)S(1)}, u32[]{:S(2)}, u32[]{:S(2)}) collective-permute-start(bf16[128,768]{1,0:T(8,128)(2,1)S(1)} %get-tuple-element.20), channel_id=1, source_target_pairs={{0,8},{1,9},{2,10},{3,11},{4,12},{5,13},{6,14},{7,15},{8,0},{9,1},... | collective-permute-start | bytes 589832 | tf_op jit(solution)/shard_map/ppermute | solution.py:139
  41.3 18.4 %collective-permute-start.13 = (bf16[128,768]{1,0:T(8,128)(2,1)S(1)}, bf16[128,768]{1,0:T(8,128)(2,1)S(1)}, u32[]{:S(2)}, u32[]{:S(2)}) collective-permute-start(bf16[128,768]{1,0:T(8,128)(2,1)S(1)} %get-tuple-element.21), channel_id=1, source_target_pairs={{0,12},{1,13},{2,14},{3,15},{4,8},{5,9},{6,10},{7,11},{8,4},{9,5},... | collective-permute-start | bytes 589832 | tf_op jit(solution)/shard_map/ppermute | solution.py:139
  42.2 18.3 %collective-permute-start.7 = (bf16[128,768]{1,0:T(8,128)(2,1)S(1)}, bf16[128,768]{1,0:T(8,128)(2,1)S(1)}, u32[]{:S(2)}, u32[]{:S(2)}) collective-permute-start(bf16[128,768]{1,0:T(8,128)(2,1)S(1)} %get-tuple-element.27), channel_id=1, source_target_pairs={{0,2},{1,3},{2,0},{3,1},{4,6},{5,7},{6,4},{7,5},{8,10},{9,11},{10,... | collective-permute-start | bytes 589832 | tf_op jit(solution)/shard_map/ppermute | solution.py:139
  43.8 18.3 %collective-permute-start.9 = (bf16[256,768]{1,0:T(8,128)(2,1)S(1)}, bf16[256,768]{1,0:T(8,128)(2,1)S(1)}, u32[]{:S(2)}, u32[]{:S(2)}) collective-permute-start(bf16[256,768]{1,0:T(8,128)(2,1)S(1)} %pad_maximum_fusion.1), channel_id=1, source_target_pairs={{0,16},{16,0},{1,17},{17,1},{2,18},{18,2},{3,19},{19,3},{4,20},{20... | collective-permute-start | bytes 1179656 | tf_op jit(solution)/shard_map/ppermute | solution.py:142
  60.6 8.0 %copy-start.5 = (f32[1,256,768]{2,1,0:T(8,128)S(1)}, f32[1,256,768]{2,1,0:T(8,128)}, u32[]{:S(2)}) copy-start(f32[1,256,768]{2,1,0:T(8,128)} %param.10) | copy-start | bytes 2359300
  60.6 8.0 %copy-start.6 = (f32[1,256,768]{2,1,0:T(8,128)S(1)}, f32[1,256,768]{2,1,0:T(8,128)}, u32[]{:S(2)}) copy-start(f32[1,256,768]{2,1,0:T(8,128)} %param.11) | copy-start | bytes 2359300
  60.6 6.5 %collective-permute-start.8 = (bf16[128,768]{1,0:T(8,128)(2,1)S(1)}, bf16[128,768]{1,0:T(8,128)(2,1)S(1)}, u32[]{:S(2)}, u32[]{:S(2)}) collective-permute-start(bf16[128,768]{1,0:T(8,128)(2,1)S(1)} %fusion.3), channel_id=1, source_target_pairs={{0,16},{16,0},{1,17},{17,1},{2,18},{18,2},{3,19},{19,3},{4,20},{20... | collective-permute-start | bytes 589832 | tf_op jit(solution)/shard_map/ppermute | solution.py:142
  62.3 6.2 %collective-permute-start.10 = (bf16[128,768]{1,0:T(8,128)(2,1)S(1)}, bf16[128,768]{1,0:T(8,128)(2,1)S(1)}, u32[]{:S(2)}, u32[]{:S(2)}) collective-permute-start(bf16[128,768]{1,0:T(8,128)(2,1)S(1)} %slice.56), channel_id=1, source_target_pairs={{0,2},{1,3},{2,0},{3,1},{4,6},{5,7},{6,4},{7,5},{8,10},{9,11},{10,... | collective-permute-start | bytes 589832 | tf_op jit(solution)/shard_map/ppermute | solution.py:139
where the time goes:
time: 70.5 us; the launch traced here: 70.2 us
  waiting for transfers between devices  42 us (60%)
  starting transfers between devices  16.1 us (23%)
  Pallas kernels  5.05 us (7%)
  local copies, waits for them, and re-layouts  3.38 us (5%)
  other arithmetic  2.93 us (4%)
  between operations  0.78 us (1%)
    ppermute x12, waiting for transfers between devices, over_cluster(): return lax.ppermute(x, 'cluster', [(i, i ^ bits) for i in range(owners)])  38.8 us
    ppermute x12, starting transfers between devices, over_cluster(): return lax.ppermute(x, 'cluster', [(i, i ^ bits) for i in range(owners)])  13 us
    pallas_call x4, Pallas kernels, kernel_call(): pl.pallas_call(kernel, out_shape=tuple((jax.ShapeDtypeStruct(shape, kind)...  5.05 us
    unnamed x14, local copies, waits for them, and re-layouts  3.31 us
    ppermute x2, waiting for transfers between devices, over_dp(): return lax.ppermute(x, 'dp', [(0, 1), (1, 0)])  3.22 us
    ppermute x2, starting transfers between devices, over_dp(): return lax.ppermute(x, 'dp', [(0, 1), (1, 0)])  3.12 us
    convert_element_type x1, other arithmetic, adam_update(): return (stepped.astype(jnp.bfloat16), first_new, second_new)  1.62 us
  transfers between devices with their start and end apart: 14, of which 8 were waited for; matrix products, arithmetic and copies ran while one was open for 2% of the time, Pallas kernels for 3%

commit v1 on v0

--- a/solution.py
+++ b/solution.py
@@ -59,55 +59,86 @@
     return jnp.where(code >= 0.0, coef, 0.0).astype(jnp.bfloat16)
 
 
-def unpack(packed_refs, rows, fanout):
-    spare = [ref[rows : rows + fanout, :].astype(jnp.float32) for ref in packed_refs]
+def unpack(packed_refs, rows):
+    spare = [ref[rows:, :].astype(jnp.float32) for ref in packed_refs]
     q = jnp.concatenate([ref[:rows, :] for ref in packed_refs], axis=0)
     listed = jnp.concatenate([x[:, :rows] for x in spare], axis=1)
     positive = jnp.concatenate([x[:, rows : 2 * rows] for x in spare], axis=1)
     return q, listed, positive
 
 
-def pack_kernel(base_ref, q_ref, listed_ref, positive_ref, out_ref):
-    rows, dim = q_ref.shape
-    fanout = listed_ref.shape[0]
-    out_ref[:rows, :] = q_ref[...]
-    ints = [listed_ref[...], positive_ref[...]]
+def load_kernel(q_hbm, listed_hbm, positive_hbm, weights_hbm, out_ref, weights_ref, ints, sems):
+    rows, dim = q_hbm.shape
+    fanout = listed_hbm.shape[0]
+    copies = [
+        pltpu.make_async_copy(q_hbm, out_ref.at[pl.ds(0, rows), :], sems.at[0]),
+        pltpu.make_async_copy(listed_hbm, ints.at[0], sems.at[1]),
+        pltpu.make_async_copy(positive_hbm, ints.at[1], sems.at[2]),
+        pltpu.make_async_copy(weights_hbm, weights_ref, sems.at[3]),
+    ]
+    for copy in copies:
+        copy.start()
+    copies[1].wait()
+    copies[2].wait()
+    parts = [ints[0], ints[1]]
     if dim > 2 * rows:
-        ints.append(jnp.zeros((fanout, dim - 2 * rows), jnp.int32))
-    spare = jnp.concatenate(ints, axis=1)
+        parts.append(jnp.zeros((fanout, dim - 2 * rows), jnp.int32))
+    spare = jnp.concatenate(parts, axis=1)
     out_ref[rows:, :] = spare.astype(jnp.float32).astype(jnp.bfloat16)
-
-
-def own_kernel(rows, base_ref, packed_ref, *refs):
-    weight_refs, (out_ref, coef_ref) = refs[:NEAR], refs[NEAR:]
+    copies[0].wait()
+    copies[3].wait()
+
+
+def load_work(queries, listed, positive, weights):
+    (rows, dim), fanout = queries.shape, listed.shape[0]
+    vmem, hbm = pl.BlockSpec(memory_space=pltpu.VMEM), pl.BlockSpec(memory_space=pltpu.HBM)
+    return pl.pallas_call(
+        load_kernel,
+        out_shape=(
+            jax.ShapeDtypeStruct((rows + fanout, dim), queries.dtype),
+            jax.ShapeDtypeStruct(weights.shape, weights.dtype),
+        ),
+        in_specs=[hbm] * 4,
+        out_specs=(vmem, vmem),
+        scratch_shapes=[
+            pltpu.VMEM((2, fanout, rows), jnp.int32),
+            pltpu.SemaphoreType.DMA((4,)),
+        ],
+        compiler_params=pltpu.CompilerParams(vmem_limit_bytes=KERNEL_VMEM),
+        name="load",
+    )(*(pltpu.with_memory_space_constraint(x, pltpu.HBM) for x in (queries, listed, positive, weights)))
+
+
+def own_kernel(rows, base_ref, *refs):
+    packed_refs, weight_refs = refs[: NEAR - 1], refs[NEAR - 1 : 2 * NEAR - 1]
+    coef_ref, out_refs = refs[2 * NEAR - 1], refs[2 * NEAR :]
     labels = weight_refs[0].shape[0]
-    q, listed, positive = unpack([packed_ref], rows, packed_ref.shape[0] - rows)
-    total = jnp.zeros(out_ref.shape, jnp.float32)
+    q, listed, positive = unpack(packed_refs, rows)
+    total = jnp.zeros(q.shape, jnp.float32)
     for j in range(NEAR):
         w = weight_refs[j][...]
         cluster = jnp.bitwise_xor(base_ref[0], j).astype(jnp.float32)
         coef = coefficients(w, q, listed, positive, cluster)
         coef_ref[j * labels : (j + 1) * labels, :] = coef
         total = total + tn_dot(coef, w)
-    out_ref[...] = total
-
-
-def grad_kernel(rows, base_ref, own_coef_ref, *refs):
+    for s, out_ref in enumerate(out_refs):
+        out_ref[...] = total[s * rows : (s + 1) * rows].astype(out_ref.dtype)
+
+
+def grad_kernel(rows, base_ref, first_coef_ref, *refs):
     packed_refs, weight_refs = refs[:NEAR], refs[NEAR : 2 * NEAR]
     coef_ref, send_ref, own_ref, beside_ref = refs[2 * NEAR :]
     labels = weight_refs[0].shape[0]
-    fanout = packed_refs[0].shape[0] - rows
-    q, listed, positive = unpack(packed_refs[1:], rows, fanout)
-    own_q = packed_refs[0][:rows, :]
+    q, listed, positive = unpack(packed_refs[NEAR - 1 :], rows)
+    all_q = jnp.concatenate([ref[:rows, :] for ref in packed_refs], axis=0)
 
     def part(j):
         cluster = jnp.bitwise_xor(base_ref[0], j).astype(jnp.float32)
         coef = coefficients(weight_refs[j][...], q, listed, positive, cluster)
         spot = slice(j * labels, (j + 1) * labels)
         coef_ref[spot, :] = coef
-        return jnp.dot(coef, q, preferred_element_type=jnp.float32) + jnp.dot(
-            own_coef_ref[spot, :], own_q, preferred_element_type=jnp.float32
-        )
+        all_coef = jnp.concatenate([first_coef_ref[spot, :], coef], axis=1)
+        return jnp.dot(all_coef, all_q, preferred_element_type=jnp.float32)
 
     send_ref[:labels, :] = part(1).astype(jnp.bfloat16)
     send_ref[labels:, :] = part(3).astype(jnp.bfloat16)
@@ -115,25 +146,22 @@
     beside_ref[...] = part(2)
 
 
-def back_kernel(rows, base_ref, coef_ref, *refs):
-    weight_refs, out_refs = refs[:NEAR], refs[NEAR:]
+def back_kernel(base_ref, coef_ref, *refs):
+    weight_refs, out_ref = refs[:NEAR], refs[NEAR]
     labels = weight_refs[0].shape[0]
-    total = jnp.zeros((coef_ref.shape[1], weight_refs[0].shape[1]), jnp.float32)
+    total = jnp.zeros(out_ref.shape, jnp.float32)
     for j in range(NEAR):
         total = total + tn_dot(coef_ref[j * labels : (j + 1) * labels, :], weight_refs[j][...])
-    for s, out_ref in enumerate(out_refs):
-        out_ref[...] = total[s * rows : (s + 1) * rows, :].astype(jnp.bfloat16)
+    out_ref[...] = total.astype(out_ref.dtype)
 
 
 def near_device(queries, shortlist, positives, weights, first_moment, second_moment):
     owners = lax.axis_size("cluster")
-    lines = owners // NEAR
-    rows, fanout = shortlist.shape
+    rows = shortlist.shape[0]
     labels, dim = weights.shape[1:]
-    half = labels // 2
-    others = (lines - 1) * rows
     base = lax.axis_index("cluster").astype(jnp.int32).reshape(1)
     low_type, wide = jnp.bfloat16, jnp.float32
+    cut = labels * 5 // 8 // 16 * 16
 
     def over_cluster(x, bits):
         return lax.ppermute(x, "cluster", [(i, i ^ bits) for i in range(owners)])
@@ -141,56 +169,50 @@
     def over_dp(x):
         return lax.ppermute(x, "dp", [(0, 1), (1, 0)])
 
-    own_weights = weights[0]
-    (packed,) = kernel_call(
-        pack_kernel,
-        [((rows + fanout, dim), low_type)],
-        [base, queries, shortlist.T, positives.T],
-        0,
-    )
-    packs = [packed] + [over_cluster(packed, NEAR * s) for s in range(1, lines)]
+    packed, own_weights = load_work(queries, shortlist.T, positives.T, weights[0])
+    q1 = over_cluster(packed, NEAR)
+    q2 = over_cluster(packed, 2 * NEAR)
+    packs = [packed, q1, q2, over_cluster(q2, NEAR)]
     weight_core = over_cluster(own_weights, 1)
     beside = over_cluster(own_weights, 2)
     near_weights = [own_weights, weight_core, beside, over_cluster(beside, 1)]
 
-    total, own_coef = kernel_call(
+    flops = 2 * rows * NEAR * labels * dim
+    block = ((rows, dim), low_type)
+    first_coef, total, *backs = kernel_call(
         functools.partial(own_kernel, rows),
-        [((rows, dim), wide), ((NEAR * labels, rows), low_type)],
-        [base, packed, *near_weights],
-        4 * rows * NEAR * labels * dim,
+        [((NEAR * labels, 3 * rows), low_type), ((rows, dim), wide), block, block],
+        [base, *packs[:3], *near_weights],
+        6 * flops,
     )
     coef, send, own, near = kernel_call(
         functools.partial(grad_kernel, rows),
         [
-            ((NEAR * labels, others), low_type),
+            ((NEAR * labels, rows), low_type),
             ((2 * labels, dim), low_type),
             ((labels, dim), wide),
             ((labels, dim), wide),
         ],
-        [base, own_coef, *packs, *near_weights],
-        4 * others * NEAR * labels * dim,
+        [base, first_coef, *packs, *near_weights],
+        5 * flops,
     )
     got = over_cluster(send, 1).astype(wide)
-    backs = kernel_call(
-        functools.partial(back_kernel, rows),
-        [((rows, dim), low_type)] * (lines - 1),
-        [base, coef, *near_weights],
-        2 * others * NEAR * labels * dim,
-    )
-    for s in range(1, lines):
-        total = total + over_cluster(backs[s - 1], NEAR * s).astype(wide)
+    backs += kernel_call(back_kernel, [block], [base, coef, *near_weights], flops)
+    for s, back in enumerate(backs, 1):
+        total = total + over_cluster(back, s * NEAR).astype(wide)
     query_grad = total.astype(low_type)
 
     own = own + got[:labels]
     near = near + got[labels:]
-    low = jnp.concatenate([own[half:], near[half:]], axis=0).astype(low_type)
-    got_top = over_cluster(near[:half].astype(low_type), 2).astype(wide)
+    low = jnp.concatenate([own[cut:], near[cut:]], axis=0).astype(low_type)
+    got_top = over_cluster(near[:cut].astype(low_type), 2).astype(wide)
     got_low = over_dp(low).astype(wide)
-    top = (own[:half] + got_top).astype(low_type)
+    top = (own[:cut] + got_top).astype(low_type)
     low = low.astype(wide) + got_low
+    low_own, low_near = low[: labels - cut], low[labels - cut :].astype(low_type)
     top = top.astype(wide) + over_dp(top).astype(wide)
-    low_own = low[:half] + over_cluster(low[half:].astype(low_type), 2).astype(wide)
-    gradient = jnp.concatenate([top, low_own], axis=0)
+    low_own = low_own + over_cluster(low_near, 2).astype(wide)
+    gradient = lax.optimization_barrier(jnp.concatenate([top, low_own], axis=0))
     new_weights, new_first, new_second = adam_update(
         own_weights, first_moment[0], second_moment[0], gradient
     )

time: 70.5 us -> 65 us (0.922)
  waiting for transfers between devices: 42 us -> 38.6 us
  local copies, waits for them, and re-layouts: 3.38 us -> 1.27 us
  starting transfers between devices: 16.1 us -> 15.1 us
  Pallas kernels: 5.05 us -> 5.95 us
    unnamed x14 -> x4, local copies, waits for them, and re-layouts: 3.31 us -> 1.2 us
    ppermute x2, waiting for transfers between devices: 3.22 us -> 1.25 us  [over_dp(): return lax.ppermute(x, 'dp', [(0, 1), (1, 0)])]
    broadcast_in_dim x0 -> x1, other arithmetic: none -> 1.83 us  [near_device(): return (new_weights[None], new_first[None], new_second[None], query_grad)]
    convert_element_type x2 -> x1, other arithmetic: 1.65 us -> 0.05 us  [near_device(): top = (own[:cut] + got_top).astype(low_type)]
    ppermute x12, waiting for transfers between devices: 38.8 us -> 37.3 us  [over_cluster(): return lax.ppermute(x, 'cluster', [(i, i ^ bits) for i in range(owners)])]
    pallas_call x0 -> x1, Pallas kernels: none -> 1.17 us  [load_work(): pl.pallas_call(load_kernel, out_shape=(jax.ShapeDtypeStruct((rows + fanou...]
    ppermute x12, starting transfers between devices: 13 us -> 12 us  [over_cluster(): return lax.ppermute(x, 'cluster', [(i, i ^ bits) for i in range(owners)])]
    pallas_call x4 -> x3, Pallas kernels: 5.05 us -> 4.78 us  [kernel_call(): pl.pallas_call(kernel, out_shape=tuple((jax.ShapeDtypeStruct(shape, kind)...]
  transfers between devices with their start and end apart: 14 -> 14, of which waited for: 8 -> 8; matrix products, arithmetic and copies ran while one was open for 2% -> 1% of each run, Pallas kernels for 3% -> 4%
where the time goes in v1:
time: 65 us; the launch traced here: 64.8 us
  waiting for transfers between devices  38.6 us (59%)
  starting transfers between devices  15.1 us (23%)
  Pallas kernels  5.95 us (9%)
  other arithmetic  3.16 us (5%)
  local copies, waits for them, and re-layouts  1.27 us (2%)
  between operations  0.77 us (1%)
    ppermute x12, waiting for transfers between devices, over_cluster(): return lax.ppermute(x, 'cluster', [(i, i ^ bits) for i in range(owners)])  37.3 us
    ppermute x12, starting transfers between devices, over_cluster(): return lax.ppermute(x, 'cluster', [(i, i ^ bits) for i in range(owners)])  12 us
    pallas_call x3, Pallas kernels, kernel_call(): pl.pallas_call(kernel, out_shape=tuple((jax.ShapeDtypeStruct(shape, kind)...  4.78 us
    ppermute x2, starting transfers between devices, over_dp(): return lax.ppermute(x, 'dp', [(0, 1), (1, 0)])  3.11 us
    broadcast_in_dim x1, other arithmetic, near_device(): return (new_weights[None], new_first[None], new_second[None], query_grad)  1.83 us
  transfers between devices with their start and end apart: 14, of which 8 were waited for; matrix products, arithmetic and copies ran while one was open for 1% of the time, Pallas kernels for 4%

profile of v1, /device:TPU:8, one launch (start us, length us, event | category | flops | bytes accessed | tf_op | source)
XLA Modules:
  0.0 64.8 jit_solution(10938409493259491756)
XLA Ops:
  0.6 1.2 %load.1 = (bf16[136,768]{1,0:T(8,128)(2,1)S(1)}, bf16[256,768]{1,0:T(8,128)(2,1)S(1)}) custom-call(bf16[128,768]{1,0:T(8,128)(2,1)} %q_hbm.1, s32[8,128]{1,0:T(8,128)} %bitcast.23, s32[8,128]{1,0:T(8,128)} %bitcast.24, bf16[256,768]{1,0:T(8,128)(2,1)} %bitcast.22), custom_call_target="tpu_custom_call" | custom-call | tf_op jit(solution)/shard_map/load/pallas_call | solution.py:95
  1.8 1.6 %collective-permute-start.3 = (bf16[256,768]{1,0:T(8,128)(2,1)S(1)}, bf16[256,768]{1,0:T(8,128)(2,1)S(1)}, u32[]{:S(2)}, u32[]{:S(2)}) collective-permute-start(bf16[256,768]{1,0:T(8,128)(2,1)S(1)} %get-tuple-element.14.refs_3_.refs_4_.refs_0_), channel_id=1, source_target_pairs={{0,2},{1,3},{2,0},{3,1},{4,6},{5,7},{6,4},{7,5},{8,10},{9,11},{10,... | collective-permute-start | bytes 1179656 | tf_op jit(solution)/shard_map/ppermute | solution.py:167
  3.4 0.0 collective-permute-start.2
  3.4 9.3 %collective-permute-done.3.refs_5_.refs_6_.refs_2_ = bf16[256,768]{1,0:T(8,128)(2,1)S(1)} collective-permute-done((bf16[256,768]{1,0:T(8,128)(2,1)S(1)}, bf16[256,768]{1,0:T(8,128)(2,1)S(1)}, u32[]{:S(2)}, u32[]{:S(2)}) %collective-permute-start.3) | collective-permute-done | bytes 393248 | tf_op jit(solution)/shard_map/ppermute | solution.py:167
  12.7 0.0 collective-permute-start.4
  12.7 2.6 %collective-permute-start.1 = (bf16[136,768]{1,0:T(8,128)(2,1)S(1)}, bf16[136,768]{1,0:T(8,128)(2,1)S(1)}, u32[]{:S(2)}, u32[]{:S(2)}) collective-permute-start(bf16[136,768]{1,0:T(8,128)(2,1)S(1)} %get-tuple-element.15.refs_0_), channel_id=1, source_target_pairs={{0,8},{1,9},{2,10},{3,11},{4,12},{5,13},{6,14},{7,15},{8,0},{9,1},... | collective-permute-start | bytes 626696 | tf_op jit(solution)/shard_map/ppermute | solution.py:167
  15.3 0.4 collective-permute-start
  15.8 9.0 %collective-permute-done.1.refs_2_ = bf16[136,768]{1,0:T(8,128)(2,1)S(1)} collective-permute-done((bf16[136,768]{1,0:T(8,128)(2,1)S(1)}, bf16[136,768]{1,0:T(8,128)(2,1)S(1)}, u32[]{:S(2)}, u32[]{:S(2)}) %collective-permute-start.1) | collective-permute-done | bytes 208928 | tf_op jit(solution)/shard_map/ppermute | solution.py:167
  24.8 1.4 %collective-permute-start.5 = (bf16[136,768]{1,0:T(8,128)(2,1)S(1)}, bf16[136,768]{1,0:T(8,128)(2,1)S(1)}, u32[]{:S(2)}, u32[]{:S(2)}) collective-permute-start(bf16[136,768]{1,0:T(8,128)(2,1)S(1)} %collective-permute-done.1.refs_2_), channel_id=1, source_target_pairs={{0,4},{1,5},{2,6},{3,7},{4,0},{5,1},{6,2},{7,3},{8,12},{9,13},{10,... | collective-permute-start | bytes 626696 | tf_op jit(solution)/shard_map/ppermute | solution.py:167
  26.2 0.0 collective-permute-done.refs_1_
  26.2 0.0 collective-permute-done.2.refs_4_.refs_5_.refs_1_
  26.2 0.0 collective-permute-done.4.refs_6_.refs_7_.refs_3_
  26.2 2.3 %shard_map.93 = (bf16[1024,384]{1,0:T(8,128)(2,1)S(1)}, f32[128,768]{1,0:T(8,128)S(1)}, bf16[128,768]{1,0:T(8,128)(2,1)S(1)}, bf16[128,768]{1,0:T(8,128)(2,1)S(1)}) custom-call(s32[1]{0:T(128)} %bitcast.4.base_ref, bf16[136,768]{1,0:T(8,128)(2,1)S(1)} %get-tuple-element.15.refs_0_, bf16[136,768]{1,0:T(8,128)(2,1)S(1)} %collective-permute-done.refs_1_, ...), custom_call_target="tpu_custom_call" | custom-call | flops 1207959552 | bytes 1048576 | tf_op jit(solution)/shard_map/pallas_call | solution.py:43
  28.5 3.4 %collective-permute-done.5.refs_3_ = bf16[136,768]{1,0:T(8,128)(2,1)S(1)} collective-permute-done((bf16[136,768]{1,0:T(8,128)(2,1)S(1)}, bf16[136,768]{1,0:T(8,128)(2,1)S(1)}, u32[]{:S(2)}, u32[]{:S(2)}) %collective-permute-start.5) | collective-permute-done | bytes 208928 | tf_op jit(solution)/shard_map/ppermute | solution.py:167
  31.9 2.0 %shard_map.94 = (bf16[1024,128]{1,0:T(8,128)(2,1)S(1)}, bf16[512,768]{1,0:T(8,128)(2,1)S(1)}, f32[256,768]{1,0:T(8,128)S(1)}, f32[256,768]{1,0:T(8,128)S(1)}) custom-call(s32[1]{0:T(128)} %bitcast.4.base_ref, bf16[1024,384]{1,0:T(8,128)(2,1)S(1)} %get-tuple-element.16.first_coef_ref, bf16[136,768]{1,0:T(8,128)(2,1)S(1)} %get-tuple-element.15.refs_0_, ...), custom_call_target="tpu_custom_call" | custom-call | flops 1006632960 | bytes 1048576 | tf_op jit(solution)/shard_map/pallas_call | solution.py:43
  34.0 0.1 collective-permute-start.6
  34.1 2.3 %collective-permute-done.6 = bf16[512,768]{1,0:T(8,128)(2,1)S(1)} collective-permute-done((bf16[512,768]{1,0:T(8,128)(2,1)S(1)}, bf16[512,768]{1,0:T(8,128)(2,1)S(1)}, u32[]{:S(2)}, u32[]{:S(2)}) %collective-permute-start.6) | collective-permute-done | bytes 786464 | tf_op jit(solution)/shard_map/ppermute | solution.py:167
  36.3 0.1 convert_element_type.46
  36.4 0.2 slice_add_fusion.1
  36.7 1.6 %collective-permute-start.7 = (bf16[160,768]{1,0:T(8,128)(2,1)S(1)}, bf16[160,768]{1,0:T(8,128)(2,1)S(1)}, u32[]{:S(2)}, u32[]{:S(2)}) collective-permute-start(bf16[160,768]{1,0:T(8,128)(2,1)S(1)} %slice.39), channel_id=1, source_target_pairs={{0,2},{1,3},{2,0},{3,1},{4,6},{5,7},{6,4},{7,5},{8,10},{9,11},{10,... | collective-permute-start | bytes 737288 | tf_op jit(solution)/shard_map/ppermute | solution.py:167
  38.3 1.6 %collective-permute-start.9 = (bf16[192,768]{1,0:T(8,128)(2,1)S(1)}, bf16[192,768]{1,0:T(8,128)(2,1)S(1)}, u32[]{:S(2)}, u32[]{:S(2)}) collective-permute-start(bf16[192,768]{1,0:T(8,128)(2,1)S(1)} %pad_maximum_fusion.1), channel_id=1, source_target_pairs={{0,16},{16,0},{1,17},{17,1},{2,18},{18,2},{3,19},{19,3},{4,20},{20... | collective-permute-start | bytes 884744 | tf_op jit(solution)/shard_map/ppermute | solution.py:170
  39.9 1.0 %collective-permute-start.11 = (bf16[128,768]{1,0:T(8,128)(2,1)S(1)}, bf16[128,768]{1,0:T(8,128)(2,1)S(1)}, u32[]{:S(2)}, u32[]{:S(2)}) collective-permute-start(bf16[128,768]{1,0:T(8,128)(2,1)S(1)} %get-tuple-element.21), channel_id=1, source_target_pairs={{0,4},{1,5},{2,6},{3,7},{4,0},{5,1},{6,2},{7,3},{8,12},{9,13},{10,... | collective-permute-start | bytes 589832 | tf_op jit(solution)/shard_map/ppermute | solution.py:167
  40.9 2.7 %collective-permute-start.12 = (bf16[128,768]{1,0:T(8,128)(2,1)S(1)}, bf16[128,768]{1,0:T(8,128)(2,1)S(1)}, u32[]{:S(2)}, u32[]{:S(2)}) collective-permute-start(bf16[128,768]{1,0:T(8,128)(2,1)S(1)} %get-tuple-element.22), channel_id=1, source_target_pairs={{0,8},{1,9},{2,10},{3,11},{4,12},{5,13},{6,14},{7,15},{8,0},{9,1},... | collective-permute-start | bytes 589832 | tf_op jit(solution)/shard_map/ppermute | solution.py:167
  43.5 0.4 shard_map.95
  44.0 0.4 collective-permute-start.13
  44.3 0.4 collective-permute-done.7
  44.8 1.6 %collective-permute-start.8 = (bf16[160,768]{1,0:T(8,128)(2,1)S(1)}, bf16[160,768]{1,0:T(8,128)(2,1)S(1)}, u32[]{:S(2)}, u32[]{:S(2)}) collective-permute-start(bf16[160,768]{1,0:T(8,128)(2,1)S(1)} %fusion.2), channel_id=1, source_target_pairs={{0,16},{16,0},{1,17},{17,1},{2,18},{18,2},{3,19},{19,3},{4,20},{20... | collective-permute-start | bytes 737288 | tf_op jit(solution)/shard_map/ppermute | solution.py:170
  46.3 1.3 %collective-permute-done.9 = bf16[192,768]{1,0:T(8,128)(2,1)S(1)} collective-permute-done((bf16[192,768]{1,0:T(8,128)(2,1)S(1)}, bf16[192,768]{1,0:T(8,128)(2,1)S(1)}, u32[]{:S(2)}, u32[]{:S(2)}) %collective-permute-start.9) | collective-permute-done | bytes 294944 | tf_op jit(solution)/shard_map/ppermute | solution.py:170
  47.6 0.1 convert_add_fusion
  47.7 0.3 collective-permute-start.10
  48.0 0.0 collective-permute-done.11
  48.1 9.0 %collective-permute-done.12 = bf16[128,768]{1,0:T(8,128)(2,1)S(1)} collective-permute-done((bf16[128,768]{1,0:T(8,128)(2,1)S(1)}, bf16[128,768]{1,0:T(8,128)(2,1)S(1)}, u32[]{:S(2)}, u32[]{:S(2)}) %collective-permute-start.12) | collective-permute-done | bytes 196640 | tf_op jit(solution)/shard_map/ppermute | solution.py:167
  57.0 3.9 %collective-permute-done.13 = bf16[128,768]{1,0:T(8,128)(2,1)S(1)} collective-permute-done((bf16[128,768]{1,0:T(8,128)(2,1)S(1)}, bf16[128,768]{1,0:T(8,128)(2,1)S(1)}, u32[]{:S(2)}, u32[]{:S(2)}) %collective-permute-start.13) | collective-permute-done | bytes 196640 | tf_op jit(solution)/shard_map/ppermute | solution.py:167
  60.9 0.8 %add_convert_fusion = bf16[128,768]{1,0:T(8,128)(2,1)} fusion(bf16[128,768]{1,0:T(8,128)(2,1)S(1)} %collective-permute-done.13, bf16[128,768]{1,0:T(8,128)(2,1)S(1)} %collective-permute-done.12, f32[128,768]{1,0:T(8,128)S(1)} %get-tuple-element.20, bf16[128,768]{1,0:T(8,128)(2,1)S(1)} %collective-permute-done.11), kind=kLoop, calls=%fused_computation.12 | loop fusion | flops 688128 | bytes 1179648 | tf_op jit(solution)/shard_map/convert_element_type | solution.py:203
  61.6 0.0 copy-start
  61.6 0.0 copy-start.1
  61.6 0.0 collective-permute-done.10
  61.7 0.0 collective-permute-done.8
  61.7 0.1 convert_add_fusion.1
  61.7 0.1 pad_maximum_fusion
  61.8 1.0 %copy-done = f32[1,256,768]{2,1,0:T(8,128)S(1)} copy-done((f32[1,256,768]{2,1,0:T(8,128)S(1)}, f32[1,256,768]{2,1,0:T(8,128)}, u32[]{:S(2)}) %copy-start) | copy-done | bytes 786456
  62.8 0.2 copy-done.1
  63.0 1.8 %fusion.5 = (f32[1,256,768]{2,1,0:T(8,128)}, bf16[1,256,768]{2,1,0:T(8,128)(2,1)}, f32[1,256,768]{2,1,0:T(8,128)}) fusion(f32[256,768]{1,0:T(8,128)S(1)} %pad_maximum_fusion, f32[1,256,768]{2,1,0:T(8,128)S(1)} %copy-done, f32[1,256,768]{2,1,0:T(8,128)S(1)} %copy-done.1, bf16[256,768]{1,0:T(8,128)(2,1)S(1)} %get-tuple-element.14.refs_3_.refs_4_.refs_0_), kind=kLoop, calls=%fused_computation.19 | loop fusion | flops 2752512 | bytes 4718592 | tf_op jit(solution)/shard_map/broadcast_in_dim | solution.py:219
  (7 shorter events, 0.2 us)
Async XLA Ops:
  1.8 10.9 %collective-permute-start.3 = (bf16[256,768]{1,0:T(8,128)(2,1)S(1)}, bf16[256,768]{1,0:T(8,128)(2,1)S(1)}, u32[]{:S(2)}, u32[]{:S(2)}) collective-permute-start(bf16[256,768]{1,0:T(8,128)(2,1)S(1)} %get-tuple-element.14.refs_3_.refs_4_.refs_0_), channel_id=1, source_target_pairs={{0,2},{1,3},{2,0},{3,1},{4,6},{5,7},{6,4},{7,5},{8,10},{9,11},{10,... | collective-permute-start | bytes 1179656 | tf_op jit(solution)/shard_map/ppermute | solution.py:167
  3.4 22.8 %collective-permute-start.2 = (bf16[256,768]{1,0:T(8,128)(2,1)S(1)}, bf16[256,768]{1,0:T(8,128)(2,1)S(1)}, u32[]{:S(2)}, u32[]{:S(2)}) collective-permute-start(bf16[256,768]{1,0:T(8,128)(2,1)S(1)} %get-tuple-element.14.refs_3_.refs_4_.refs_0_), channel_id=1, source_target_pairs={{0,1},{1,0},{2,3},{3,2},{4,5},{5,4},{6,7},{7,6},{8,9},{9,8},{10,11... | collective-permute-start | bytes 1179656 | tf_op jit(solution)/shard_map/ppermute | solution.py:167
  12.7 13.5 %collective-permute-start.4 = (bf16[256,768]{1,0:T(8,128)(2,1)S(1)}, bf16[256,768]{1,0:T(8,128)(2,1)S(1)}, u32[]{:S(2)}, u32[]{:S(2)}) collective-permute-start(bf16[256,768]{1,0:T(8,128)(2,1)S(1)} %collective-permute-done.3.refs_5_.refs_6_.refs_2_), channel_id=1, source_target_pairs={{0,1},{1,0},{2,3},{3,2},{4,5},{5,4},{6,7},{7,6},{8,9},{9,8},{10,11... | collective-permute-start | bytes 1179656 | tf_op jit(solution)/shard_map/ppermute | solution.py:167
  12.7 12.1 %collective-permute-start.1 = (bf16[136,768]{1,0:T(8,128)(2,1)S(1)}, bf16[136,768]{1,0:T(8,128)(2,1)S(1)}, u32[]{:S(2)}, u32[]{:S(2)}) collective-permute-start(bf16[136,768]{1,0:T(8,128)(2,1)S(1)} %get-tuple-element.15.refs_0_), channel_id=1, source_target_pairs={{0,8},{1,9},{2,10},{3,11},{4,12},{5,13},{6,14},{7,15},{8,0},{9,1},... | collective-permute-start | bytes 626696 | tf_op jit(solution)/shard_map/ppermute | solution.py:167
  15.3 10.9 %collective-permute-start = (bf16[136,768]{1,0:T(8,128)(2,1)S(1)}, bf16[136,768]{1,0:T(8,128)(2,1)S(1)}, u32[]{:S(2)}, u32[]{:S(2)}) collective-permute-start(bf16[136,768]{1,0:T(8,128)(2,1)S(1)} %get-tuple-element.15.refs_0_), channel_id=1, source_target_pairs={{0,4},{1,5},{2,6},{3,7},{4,0},{5,1},{6,2},{7,3},{8,12},{9,13},{10,... | collective-permute-start | bytes 626696 | tf_op jit(solution)/shard_map/ppermute | solution.py:167
  24.8 7.1 %collective-permute-start.5 = (bf16[136,768]{1,0:T(8,128)(2,1)S(1)}, bf16[136,768]{1,0:T(8,128)(2,1)S(1)}, u32[]{:S(2)}, u32[]{:S(2)}) collective-permute-start(bf16[136,768]{1,0:T(8,128)(2,1)S(1)} %collective-permute-done.1.refs_2_), channel_id=1, source_target_pairs={{0,4},{1,5},{2,6},{3,7},{4,0},{5,1},{6,2},{7,3},{8,12},{9,13},{10,... | collective-permute-start | bytes 626696 | tf_op jit(solution)/shard_map/ppermute | solution.py:167
  34.0 2.4 %collective-permute-start.6 = (bf16[512,768]{1,0:T(8,128)(2,1)S(1)}, bf16[512,768]{1,0:T(8,128)(2,1)S(1)}, u32[]{:S(2)}, u32[]{:S(2)}) collective-permute-start(bf16[512,768]{1,0:T(8,128)(2,1)S(1)} %get-tuple-element.18), channel_id=1, source_target_pairs={{0,1},{1,0},{2,3},{3,2},{4,5},{5,4},{6,7},{7,6},{8,9},{9,8},{10,11... | collective-permute-start | bytes 2359304 | tf_op jit(solution)/shard_map/ppermute | solution.py:167
  36.7 8.1 %collective-permute-start.7 = (bf16[160,768]{1,0:T(8,128)(2,1)S(1)}, bf16[160,768]{1,0:T(8,128)(2,1)S(1)}, u32[]{:S(2)}, u32[]{:S(2)}) collective-permute-start(bf16[160,768]{1,0:T(8,128)(2,1)S(1)} %slice.39), channel_id=1, source_target_pairs={{0,2},{1,3},{2,0},{3,1},{4,6},{5,7},{6,4},{7,5},{8,10},{9,11},{10,... | collective-permute-start | bytes 737288 | tf_op jit(solution)/shard_map/ppermute | solution.py:167
  38.3 9.3 %collective-permute-start.9 = (bf16[192,768]{1,0:T(8,128)(2,1)S(1)}, bf16[192,768]{1,0:T(8,128)(2,1)S(1)}, u32[]{:S(2)}, u32[]{:S(2)}) collective-permute-start(bf16[192,768]{1,0:T(8,128)(2,1)S(1)} %pad_maximum_fusion.1), channel_id=1, source_target_pairs={{0,16},{16,0},{1,17},{17,1},{2,18},{18,2},{3,19},{19,3},{4,20},{20... | collective-permute-start | bytes 884744 | tf_op jit(solution)/shard_map/ppermute | solution.py:170
  39.9 8.2 %collective-permute-start.11 = (bf16[128,768]{1,0:T(8,128)(2,1)S(1)}, bf16[128,768]{1,0:T(8,128)(2,1)S(1)}, u32[]{:S(2)}, u32[]{:S(2)}) collective-permute-start(bf16[128,768]{1,0:T(8,128)(2,1)S(1)} %get-tuple-element.21), channel_id=1, source_target_pairs={{0,4},{1,5},{2,6},{3,7},{4,0},{5,1},{6,2},{7,3},{8,12},{9,13},{10,... | collective-permute-start | bytes 589832 | tf_op jit(solution)/shard_map/ppermute | solution.py:167
  40.9 16.2 %collective-permute-start.12 = (bf16[128,768]{1,0:T(8,128)(2,1)S(1)}, bf16[128,768]{1,0:T(8,128)(2,1)S(1)}, u32[]{:S(2)}, u32[]{:S(2)}) collective-permute-start(bf16[128,768]{1,0:T(8,128)(2,1)S(1)} %get-tuple-element.22), channel_id=1, source_target_pairs={{0,8},{1,9},{2,10},{3,11},{4,12},{5,13},{6,14},{7,15},{8,0},{9,1},... | collective-permute-start | bytes 589832 | tf_op jit(solution)/shard_map/ppermute | solution.py:167
  44.0 16.9 %collective-permute-start.13 = (bf16[128,768]{1,0:T(8,128)(2,1)S(1)}, bf16[128,768]{1,0:T(8,128)(2,1)S(1)}, u32[]{:S(2)}, u32[]{:S(2)}) collective-permute-start(bf16[128,768]{1,0:T(8,128)(2,1)S(1)} %shard_map.95), channel_id=1, source_target_pairs={{0,12},{1,13},{2,14},{3,15},{4,8},{5,9},{6,10},{7,11},{8,4},{9,5},... | collective-permute-start | bytes 589832 | tf_op jit(solution)/shard_map/ppermute | solution.py:167
  44.8 16.9 %collective-permute-start.8 = (bf16[160,768]{1,0:T(8,128)(2,1)S(1)}, bf16[160,768]{1,0:T(8,128)(2,1)S(1)}, u32[]{:S(2)}, u32[]{:S(2)}) collective-permute-start(bf16[160,768]{1,0:T(8,128)(2,1)S(1)} %fusion.2), channel_id=1, source_target_pairs={{0,16},{16,0},{1,17},{17,1},{2,18},{18,2},{3,19},{19,3},{4,20},{20... | collective-permute-start | bytes 737288 | tf_op jit(solution)/shard_map/ppermute | solution.py:170
  47.7 14.0 %collective-permute-start.10 = (bf16[96,768]{1,0:T(8,128)(2,1)S(1)}, bf16[96,768]{1,0:T(8,128)(2,1)S(1)}, u32[]{:S(2)}, u32[]{:S(2)}) collective-permute-start(bf16[96,768]{1,0:T(8,128)(2,1)S(1)} %slice.54), channel_id=1, source_target_pairs={{0,2},{1,3},{2,0},{3,1},{4,6},{5,7},{6,4},{7,5},{8,10},{9,11},{10,... | collective-permute-start | bytes 442376 | tf_op jit(solution)/shard_map/ppermute | solution.py:167
  61.6 1.1 %copy-start = (f32[1,256,768]{2,1,0:T(8,128)S(1)}, f32[1,256,768]{2,1,0:T(8,128)}, u32[]{:S(2)}) copy-start(f32[1,256,768]{2,1,0:T(8,128)} %param.11) | copy-start | bytes 2359300
  61.6 1.4 %copy-start.1 = (f32[1,256,768]{2,1,0:T(8,128)S(1)}, f32[1,256,768]{2,1,0:T(8,128)}, u32[]{:S(2)}) copy-start(f32[1,256,768]{2,1,0:T(8,128)} %param.10) | copy-start | bytes 2359300

commit v2 on v1

--- a/solution.py
+++ b/solution.py
@@ -16,6 +16,7 @@
 
 NEAR = 4
 KERNEL_VMEM = 16 << 20
+PIECE = 48
 
 
 def adam_update(cluster_weights, first_moment, second_moment, gradient):
@@ -37,14 +38,19 @@
     return lax.dot_general(a, b, (((1,), (1,)), ((), ())), preferred_element_type=jnp.float32)
 
 
-def kernel_call(kernel, outs, args, flops):
-    vmem = pl.BlockSpec(memory_space=pltpu.VMEM)
-    specs = [pl.BlockSpec(memory_space=pltpu.SMEM)] + [vmem] * (len(args) - 1)
+def kernel_call(kernel, outs, args, flops, far=0):
+    vmem, hbm = pl.BlockSpec(memory_space=pltpu.VMEM), pl.BlockSpec(memory_space=pltpu.HBM)
+    specs = [pl.BlockSpec(memory_space=pltpu.SMEM)] + [hbm] * far + [vmem] * (len(args) - 1 - far)
+    args = [
+        pltpu.with_memory_space_constraint(x, pltpu.HBM) if spec is hbm else x
+        for x, spec in zip(args, specs)
+    ]
     return pl.pallas_call(
         kernel,
         out_shape=tuple(jax.ShapeDtypeStruct(shape, kind) for shape, kind in outs),
         in_specs=specs,
         out_specs=tuple([vmem] * len(outs)),
+        scratch_shapes=[pltpu.SemaphoreType.DMA((far,))] if far else [],
         compiler_params=pltpu.CompilerParams(vmem_limit_bytes=KERNEL_VMEM),
         cost_estimate=pl.CostEstimate(flops=flops, bytes_accessed=1 << 20, transcendentals=0),
     )(*args)
@@ -109,50 +115,145 @@
     )(*(pltpu.with_memory_space_constraint(x, pltpu.HBM) for x in (queries, listed, positive, weights)))
 
 
-def own_kernel(rows, base_ref, *refs):
-    packed_refs, weight_refs = refs[: NEAR - 1], refs[NEAR - 1 : 2 * NEAR - 1]
-    coef_ref, out_refs = refs[2 * NEAR - 1], refs[2 * NEAR :]
+def own_kernel(rows, near, base_ref, *refs):
+    blocks = NEAR - 1
+    packed_refs, weight_refs = refs[:blocks], refs[blocks : blocks + len(near)]
+    so_far_ref, coef_ref, out_refs = None, refs[blocks + len(near)], refs[blocks + len(near) + 1 :]
+    if len(out_refs) > 1:
+        so_far_ref, coef_ref, out_refs = coef_ref, out_refs[0], out_refs[1:]
     labels = weight_refs[0].shape[0]
     q, listed, positive = unpack(packed_refs, rows)
-    total = jnp.zeros(q.shape, jnp.float32)
-    for j in range(NEAR):
-        w = weight_refs[j][...]
+    total = jnp.zeros(q.shape, jnp.float32) if so_far_ref is None else so_far_ref[...]
+    for at, j in enumerate(near):
+        w = weight_refs[at][...]
         cluster = jnp.bitwise_xor(base_ref[0], j).astype(jnp.float32)
         coef = coefficients(w, q, listed, positive, cluster)
-        coef_ref[j * labels : (j + 1) * labels, :] = coef
+        coef_ref[at * labels : (at + 1) * labels, :] = coef
         total = total + tn_dot(coef, w)
+    if len(out_refs) == 1:
+        out_refs[0][...] = total
+        return
     for s, out_ref in enumerate(out_refs):
         out_ref[...] = total[s * rows : (s + 1) * rows].astype(out_ref.dtype)
 
 
-def grad_kernel(rows, base_ref, first_coef_ref, *refs):
-    packed_refs, weight_refs = refs[:NEAR], refs[NEAR : 2 * NEAR]
-    coef_ref, send_ref, own_ref, beside_ref = refs[2 * NEAR :]
-    labels = weight_refs[0].shape[0]
+def first_kernel(rows, base_ref, first_hbm, second_hbm, *refs):
+    *work, first_ref, second_ref, sems = refs
+    copies = [
+        pltpu.make_async_copy(first_hbm, first_ref, sems.at[0]),
+        pltpu.make_async_copy(second_hbm, second_ref, sems.at[1]),
+    ]
+    for copy in copies:
+        copy.start()
+    own_kernel(rows, (0, 1), base_ref, *work)
+    for copy in copies:
+        copy.wait()
+
+
+def grad_part(rows, j, base_ref, weight_ref, first_coef, packed_refs):
     q, listed, positive = unpack(packed_refs[NEAR - 1 :], rows)
     all_q = jnp.concatenate([ref[:rows, :] for ref in packed_refs], axis=0)
-
-    def part(j):
-        cluster = jnp.bitwise_xor(base_ref[0], j).astype(jnp.float32)
-        coef = coefficients(weight_refs[j][...], q, listed, positive, cluster)
-        spot = slice(j * labels, (j + 1) * labels)
-        coef_ref[spot, :] = coef
-        all_coef = jnp.concatenate([first_coef_ref[spot, :], coef], axis=1)
-        return jnp.dot(all_coef, all_q, preferred_element_type=jnp.float32)
-
-    send_ref[:labels, :] = part(1).astype(jnp.bfloat16)
-    send_ref[labels:, :] = part(3).astype(jnp.bfloat16)
-    own_ref[...] = part(0)
-    beside_ref[...] = part(2)
-
-
-def back_kernel(base_ref, coef_ref, *refs):
-    weight_refs, out_ref = refs[:NEAR], refs[NEAR]
-    labels = weight_refs[0].shape[0]
-    total = jnp.zeros(out_ref.shape, jnp.float32)
-    for j in range(NEAR):
-        total = total + tn_dot(coef_ref[j * labels : (j + 1) * labels, :], weight_refs[j][...])
-    out_ref[...] = total.astype(out_ref.dtype)
+    cluster = jnp.bitwise_xor(base_ref[0], j).astype(jnp.float32)
+    coef = coefficients(weight_ref[...], q, listed, positive, cluster)
+    all_coef = jnp.concatenate([first_coef, coef], axis=1)
+    return coef, jnp.dot(all_coef, all_q, preferred_element_type=jnp.float32)
+
+
+def sent_kernel(rows, labels, base_ref, far_coef_ref, weight_ref, *refs):
+    packed_refs, (coef_ref, send_ref) = refs[:NEAR], refs[NEAR:]
+    coef_ref[...], part = grad_part(
+        rows, 3, base_ref, weight_ref, far_coef_ref[labels:, :], packed_refs
+    )
+    send_ref[...] = part.astype(send_ref.dtype)
+
+
+def middle_kernel(rows, labels, base_ref, near_coef_ref, far_coef_ref, *refs):
+    (weight1_ref, weight2_ref), packed_refs = refs[:2], refs[2 : NEAR + 2]
+    coef1_ref, coef2_ref, send_ref, beside_ref = refs[NEAR + 2 :]
+    coef1_ref[...], part = grad_part(
+        rows, 1, base_ref, weight1_ref, near_coef_ref[labels:, :], packed_refs
+    )
+    send_ref[...] = part.astype(send_ref.dtype)
+    coef2_ref[...], beside_ref[...] = grad_part(
+        rows, 2, base_ref, weight2_ref, far_coef_ref[:labels, :], packed_refs
+    )
+
+
+def last_kernel(rows, labels, base_ref, near_coef_ref, *refs):
+    coef_refs, weight_refs = refs[: NEAR - 1], refs[NEAR - 1 : 2 * NEAR - 1]
+    packed_refs, (own_ref, back_ref) = refs[2 * NEAR - 1 : 3 * NEAR - 1], refs[3 * NEAR - 1 :]
+    coef, own_ref[...] = grad_part(
+        rows, 0, base_ref, weight_refs[0], near_coef_ref[:labels, :], packed_refs
+    )
+    total = tn_dot(coef, weight_refs[0][...])
+    for coef_ref, weight_ref in zip(coef_refs, weight_refs[1:]):
+        total = total + tn_dot(coef_ref[...], weight_ref[...])
+    back_ref[...] = total.astype(back_ref.dtype)
+
+
+def sum_kernel(base_ref, mine_ref, got_ref, out_ref):
+    out_ref[...] = (mine_ref[...] + got_ref[...].astype(jnp.float32)).astype(out_ref.dtype)
+
+
+def beside_kernel(base_ref, mine_ref, got_ref, top_ref, low_ref):
+    cut = top_ref.shape[0]
+    total = mine_ref[...] + got_ref[...].astype(jnp.float32)
+    top_ref[...] = total[:cut].astype(top_ref.dtype)
+    low_ref[...] = total[cut:].astype(low_ref.dtype)
+
+
+def mine_kernel(base_ref, mine_ref, got_ref, low_beside_ref, top_ref, low_ref):
+    cut = top_ref.shape[0]
+    rest = low_beside_ref.shape[0]
+    total = mine_ref[...] + got_ref[...].astype(jnp.float32)
+    top_ref[...] = total[:cut]
+    low_ref[:rest, :] = total[cut:].astype(low_ref.dtype)
+    low_ref[rest:, :] = low_beside_ref[...]
+
+
+def adam_kernel(start, pieces, mine_ref, got_ref, weights_ref, first_ref, second_ref, *refs):
+    *outs, sems = refs[-7:]
+    outs_hbm, scratch = outs[:3], outs[3:]
+    copies, at = [], 0
+    for piece, rows in enumerate(pieces):
+        here, there = slice(at, at + rows), slice(start + at, start + at + rows)
+        gradient = mine_ref[here, :].astype(jnp.float32) + got_ref[here, :].astype(jnp.float32)
+        new = adam_update(
+            weights_ref[there, :], first_ref[there, :], second_ref[there, :], gradient
+        )
+        for which, value in enumerate(new):
+            scratch[which][here, :] = value
+            copies.append(
+                pltpu.make_async_copy(
+                    scratch[which].at[pl.ds(at, rows), :],
+                    outs_hbm[which].at[pl.ds(start + at, rows), :],
+                    sems.at[which, piece],
+                )
+            )
+            copies[-1].start()
+        at += rows
+    for copy in copies:
+        copy.wait()
+
+
+def adam_work(start, mine, got, old, earlier):
+    rows, dim = mine.shape
+    pieces = [min(PIECE, rows - at) for at in range(0, rows, PIECE)]
+    vmem, hbm = pl.BlockSpec(memory_space=pltpu.VMEM), pl.BlockSpec(memory_space=pltpu.HBM)
+    earlier = [pltpu.with_memory_space_constraint(x, pltpu.HBM) for x in earlier]
+    return pl.pallas_call(
+        functools.partial(adam_kernel, start, pieces),
+        out_shape=tuple(pltpu.HBM(x.shape, x.dtype) for x in old),
+        in_specs=[vmem] * 5 + [hbm] * len(earlier),
+        out_specs=(hbm, hbm, hbm),
+        scratch_shapes=[pltpu.VMEM((rows, dim), x.dtype) for x in old]
+        + [pltpu.SemaphoreType.DMA((3, len(pieces)))],
+        input_output_aliases={5 + i: i for i in range(len(earlier))},
+        compiler_params=pltpu.CompilerParams(vmem_limit_bytes=KERNEL_VMEM),
+        cost_estimate=pl.CostEstimate(
+            flops=20 * rows * dim, bytes_accessed=20 * rows * dim, transcendentals=rows * dim
+        ),
+    )(mine, got, *old, *earlier)
 
 
 def near_device(queries, shortlist, positives, weights, first_moment, second_moment):
@@ -161,7 +262,7 @@
     labels, dim = weights.shape[1:]
     base = lax.axis_index("cluster").astype(jnp.int32).reshape(1)
     low_type, wide = jnp.bfloat16, jnp.float32
-    cut = labels * 5 // 8 // 16 * 16
+    cut = labels * 11 // 16 // 16 * 16
 
     def over_cluster(x, bits):
         return lax.ppermute(x, "cluster", [(i, i ^ bits) for i in range(owners)])
@@ -177,45 +278,67 @@
     beside = over_cluster(own_weights, 2)
     near_weights = [own_weights, weight_core, beside, over_cluster(beside, 1)]
 
-    flops = 2 * rows * NEAR * labels * dim
-    block = ((rows, dim), low_type)
-    first_coef, total, *backs = kernel_call(
-        functools.partial(own_kernel, rows),
-        [((NEAR * labels, 3 * rows), low_type), ((rows, dim), wide), block, block],
-        [base, *packs[:3], *near_weights],
-        6 * flops,
-    )
-    coef, send, own, near = kernel_call(
-        functools.partial(grad_kernel, rows),
-        [
-            ((NEAR * labels, rows), low_type),
-            ((2 * labels, dim), low_type),
-            ((labels, dim), wide),
-            ((labels, dim), wide),
-        ],
-        [base, first_coef, *packs, *near_weights],
-        5 * flops,
-    )
-    got = over_cluster(send, 1).astype(wide)
-    backs += kernel_call(back_kernel, [block], [base, coef, *near_weights], flops)
+    flops = 2 * rows * labels * dim
+    block, coefs = ((rows, dim), low_type), ((2 * labels, 3 * rows), low_type)
+    moment = ((labels, dim), wide)
+    near_coef, so_far, old_first, old_second = kernel_call(
+        functools.partial(first_kernel, rows),
+        [coefs, ((3 * rows, dim), wide), moment, moment],
+        [base, first_moment[0], second_moment[0], *packs[:3], *near_weights[:2]],
+        12 * flops,
+        far=2,
+    )
+    far_coef, total, *backs = kernel_call(
+        functools.partial(own_kernel, rows, (2, 3)),
+        [coefs, ((rows, dim), wide), block, block],
+        [base, *packs[:3], *near_weights[2:], so_far],
+        12 * flops,
+    )
+    last_coef, part = ((labels, rows), low_type), ((labels, dim), low_type)
+    kernel = lambda body, outs, args, times: kernel_call(
+        functools.partial(body, rows, labels), outs, [base, *args], times * flops
+    )
+    coef3, send3 = kernel(sent_kernel, [last_coef, part], [far_coef, near_weights[3], *packs], 5)
+    got3 = over_cluster(send3, 1)
+    coef1, coef2, send1, near = kernel(
+        middle_kernel,
+        [last_coef, last_coef, part, ((labels, dim), wide)],
+        [near_coef, far_coef, *near_weights[1:3], *packs],
+        10,
+    )
+    got1 = over_cluster(send1, 1)
+    top_near, low_near = kernel_call(
+        beside_kernel,
+        [((cut, dim), low_type), ((labels - cut, dim), low_type)],
+        [base, near, got3],
+        labels * dim,
+    )
+    got_top = over_cluster(top_near, 2)
+    own, back = kernel(
+        last_kernel,
+        [((labels, dim), wide), block],
+        [near_coef, coef1, coef2, coef3, *near_weights, *packs],
+        9,
+    )
+    backs.append(back)
+    own_top, low = kernel_call(
+        mine_kernel,
+        [((cut, dim), wide), ((2 * (labels - cut), dim), low_type)],
+        [base, own, got1, low_near],
+        labels * dim,
+    )
+    got_low = over_dp(low).astype(wide)
     for s, back in enumerate(backs, 1):
         total = total + over_cluster(back, s * NEAR).astype(wide)
     query_grad = total.astype(low_type)
 
-    own = own + got[:labels]
-    near = near + got[labels:]
-    low = jnp.concatenate([own[cut:], near[cut:]], axis=0).astype(low_type)
-    got_top = over_cluster(near[:cut].astype(low_type), 2).astype(wide)
-    got_low = over_dp(low).astype(wide)
-    top = (own[:cut] + got_top).astype(low_type)
+    (top,) = kernel_call(sum_kernel, [((cut, dim), low_type)], [base, own_top, got_top], cut * dim)
     low = low.astype(wide) + got_low
     low_own, low_near = low[: labels - cut], low[labels - cut :].astype(low_type)
-    top = top.astype(wide) + over_dp(top).astype(wide)
-    low_own = low_own + over_cluster(low_near, 2).astype(wide)
-    gradient = lax.optimization_barrier(jnp.concatenate([top, low_own], axis=0))
-    new_weights, new_first, new_second = adam_update(
-        own_weights, first_moment[0], second_moment[0], gradient
-    )
+    got_top, got_low = over_dp(top), over_cluster(low_near, 2)
+    old = (own_weights, old_first, old_second)
+    partly = adam_work(cut, low_own, got_low, old, ())
+    new_weights, new_first, new_second = adam_work(0, top, got_top, old, partly)
     return (new_weights[None], new_first[None], new_second[None], query_grad)
 
 

time: 65 us -> 62.8 us (0.966)
  waiting for transfers between devices: 38.6 us -> 35.3 us
  Pallas kernels: 5.95 us -> 8.96 us
  other arithmetic: 3.16 us -> 0.83 us
  starting transfers between devices: 15.1 us -> 16.7 us
  local copies, waits for them, and re-layouts: 1.27 us -> 0.03 us
    pallas_call x0 -> x2, Pallas kernels: none -> 2.3 us  [adam_work(): pl.pallas_call(functools.partial(adam_kernel, start, pieces), out_shape=t...]
    ppermute x12 -> x13, waiting for transfers between devices: 37.3 us -> 35.2 us  [over_cluster(): return lax.ppermute(x, 'cluster', [(i, i ^ bits) for i in range(owners)])]
    broadcast_in_dim x1 -> x0, other arithmetic: 1.83 us -> none  [near_device(): return (new_weights[None], new_first[None], new_second[None], query_grad)]
    ppermute x12 -> x13, starting transfers between devices: 12 us -> 13.6 us  [over_cluster(): return lax.ppermute(x, 'cluster', [(i, i ^ bits) for i in range(owners)])]
    unnamed x4 -> x0, local copies, waits for them, and re-layouts: 1.2 us -> none
    ppermute x2, waiting for transfers between devices: 1.25 us -> 0.14 us  [over_dp(): return lax.ppermute(x, 'dp', [(0, 1), (1, 0)])]
    pallas_call x3 -> x8, Pallas kernels: 4.78 us -> 5.49 us  [kernel_call(): pl.pallas_call(kernel, out_shape=tuple((jax.ShapeDtypeStruct(shape, kind)...]
  transfers between devices with their start and end apart: 14 -> 15, of which waited for: 8 -> 9; matrix products, arithmetic and copies ran while one was open for 1% -> 1% of each run, Pallas kernels for 4% -> 9%
where the time goes in v2:
time: 62.8 us; the launch traced here: 62.6 us
  waiting for transfers between devices  35.3 us (56%)
  starting transfers between devices  16.7 us (27%)
  Pallas kernels  8.96 us (14%)
  other arithmetic  0.83 us (1%)
  between operations  0.76 us (1%)
    ppermute x13, waiting for transfers between devices, over_cluster(): return lax.ppermute(x, 'cluster', [(i, i ^ bits) for i in range(owners)])  35.2 us
    ppermute x13, starting transfers between devices, over_cluster(): return lax.ppermute(x, 'cluster', [(i, i ^ bits) for i in range(owners)])  13.6 us
    pallas_call x8, Pallas kernels, kernel_call(): pl.pallas_call(kernel, out_shape=tuple((jax.ShapeDtypeStruct(shape, kind)...  5.49 us
    ppermute x2, starting transfers between devices, over_dp(): return lax.ppermute(x, 'dp', [(0, 1), (1, 0)])  3.11 us
    pallas_call x2, Pallas kernels, adam_work(): pl.pallas_call(functools.partial(adam_kernel, start, pieces), out_shape=t...  2.3 us
  transfers between devices with their start and end apart: 15, of which 9 were waited for; matrix products, arithmetic and copies ran while one was open for 1% of the time, Pallas kernels for 9%

profile of v2, /device:TPU:8, one launch (start us, length us, event | category | flops | bytes accessed | tf_op | source)
XLA Modules:
  0.0 62.6 jit_solution(17314953598651811849)
XLA Ops:
  0.6 1.2 %load.1 = (bf16[136,768]{1,0:T(8,128)(2,1)S(1)}, bf16[256,768]{1,0:T(8,128)(2,1)S(1)}) custom-call(bf16[128,768]{1,0:T(8,128)(2,1)} %q_hbm.1, s32[8,128]{1,0:T(8,128)} %bitcast.15, s32[8,128]{1,0:T(8,128)} %bitcast.16, bf16[256,768]{1,0:T(8,128)(2,1)} %bitcast.14), custom_call_target="tpu_custom_call" | custom-call | tf_op jit(solution)/shard_map/load/pallas_call | solution.py:101
  1.8 1.6 %collective-permute-start.3 = (bf16[256,768]{1,0:T(8,128)(2,1)S(1)}, bf16[256,768]{1,0:T(8,128)(2,1)S(1)}, u32[]{:S(2)}, u32[]{:S(2)}) collective-permute-start(bf16[256,768]{1,0:T(8,128)(2,1)S(1)} %get-tuple-element.33.refs_3_.weights_ref), channel_id=1, source_target_pairs={{0,2},{1,3},{2,0},{3,1},{4,6},{5,7},{6,4},{7,5},{8,10},{9,11},{10,... | collective-permute-start | bytes 1179656 | tf_op jit(solution)/shard_map/ppermute | solution.py:268
  3.4 0.0 collective-permute-start.2
  3.4 9.3 %collective-permute-done.3.refs_3_.refs_1_.refs_5_ = bf16[256,768]{1,0:T(8,128)(2,1)S(1)} collective-permute-done((bf16[256,768]{1,0:T(8,128)(2,1)S(1)}, bf16[256,768]{1,0:T(8,128)(2,1)S(1)}, u32[]{:S(2)}, u32[]{:S(2)}) %collective-permute-start.3) | collective-permute-done | bytes 393248 | tf_op jit(solution)/shard_map/ppermute | solution.py:268
  12.7 0.0 collective-permute-start.4
  12.7 2.6 %collective-permute-start.1 = (bf16[136,768]{1,0:T(8,128)(2,1)S(1)}, bf16[136,768]{1,0:T(8,128)(2,1)S(1)}, u32[]{:S(2)}, u32[]{:S(2)}) collective-permute-start(bf16[136,768]{1,0:T(8,128)(2,1)S(1)} %get-tuple-element.32.refs_0_.refs_2_.refs_7_), channel_id=1, source_target_pairs={{0,8},{1,9},{2,10},{3,11},{4,12},{5,13},{6,14},{7,15},{8,0},{9,1},... | collective-permute-start | bytes 626696 | tf_op jit(solution)/shard_map/ppermute | solution.py:268
  15.3 0.4 collective-permute-start
  15.8 9.0 %collective-permute-done.1.refs_2_.refs_4_.refs_9_ = bf16[136,768]{1,0:T(8,128)(2,1)S(1)} collective-permute-done((bf16[136,768]{1,0:T(8,128)(2,1)S(1)}, bf16[136,768]{1,0:T(8,128)(2,1)S(1)}, u32[]{:S(2)}, u32[]{:S(2)}) %collective-permute-start.1) | collective-permute-done | bytes 208928 | tf_op jit(solution)/shard_map/ppermute | solution.py:268
  24.8 1.4 %collective-permute-start.5 = (bf16[136,768]{1,0:T(8,128)(2,1)S(1)}, bf16[136,768]{1,0:T(8,128)(2,1)S(1)}, u32[]{:S(2)}, u32[]{:S(2)}) collective-permute-start(bf16[136,768]{1,0:T(8,128)(2,1)S(1)} %collective-permute-done.1.refs_2_.refs_4_.refs_9_), channel_id=1, source_target_pairs={{0,4},{1,5},{2,6},{3,7},{4,0},{5,1},{6,2},{7,3},{8,12},{9,13},{10,... | collective-permute-start | bytes 626696 | tf_op jit(solution)/shard_map/ppermute | solution.py:268
  26.2 0.0 collective-permute-done.refs_1_.refs_3_.refs_8_
  26.2 0.0 collective-permute-done.2.refs_4_.refs_0_
  26.2 1.4 %shard_map.93 = (bf16[512,384]{1,0:T(8,128)(2,1)S(1)}, f32[384,768]{1,0:T(8,128)S(1)}, f32[256,768]{1,0:T(8,128)S(1)}, f32[256,768]{1,0:T(8,128)S(1)}) custom-call(s32[1]{0:T(128)} %bitcast.base_ref, f32[256,768]{1,0:T(8,128)} %bitcast.9, f32[256,768]{1,0:T(8,128)} %bitcast.10, bf16[136,768]{1,0:T(8,128)(2,1)S(1)} %get-tuple-element.32.refs_0_.refs_2_.refs_7_, ...), custom_call_target="tpu_custom_call" | custom-call | flops 603979776 | bytes 1048576 | tf_op jit(solution)/shard_map/pallas_call | solution.py:48
  27.6 0.0 collective-permute-done.4.refs_4_.weight_ref.refs_6_
  27.6 1.3 %shard_map.94 = (bf16[512,384]{1,0:T(8,128)(2,1)S(1)}, f32[128,768]{1,0:T(8,128)S(1)}, bf16[128,768]{1,0:T(8,128)(2,1)S(1)}, bf16[128,768]{1,0:T(8,128)(2,1)S(1)}) custom-call(s32[1]{0:T(128)} %bitcast.base_ref, bf16[136,768]{1,0:T(8,128)(2,1)S(1)} %get-tuple-element.32.refs_0_.refs_2_.refs_7_, ...), custom_call_target="tpu_custom_call" | custom-call | flops 603979776 | bytes 1048576 | tf_op jit(solution)/shard_map/pallas_call | solution.py:48
  28.9 3.0 %collective-permute-done.5.refs_5_.refs_3_.refs_10_ = bf16[136,768]{1,0:T(8,128)(2,1)S(1)} collective-permute-done((bf16[136,768]{1,0:T(8,128)(2,1)S(1)}, bf16[136,768]{1,0:T(8,128)(2,1)S(1)}, u32[]{:S(2)}, u32[]{:S(2)}) %collective-permute-start.5) | collective-permute-done | bytes 208928 | tf_op jit(solution)/shard_map/ppermute | solution.py:268
  31.9 0.6 shard_map.96
  32.5 0.1 collective-permute-start.7
  32.6 1.1 %shard_map.95 = (bf16[256,128]{1,0:T(8,128)(2,1)S(1)}, bf16[256,128]{1,0:T(8,128)(2,1)S(1)}, bf16[256,768]{1,0:T(8,128)(2,1)S(1)}, f32[256,768]{1,0:T(8,128)S(1)}) custom-call(s32[1]{0:T(128)} %bitcast.base_ref, bf16[512,384]{1,0:T(8,128)(2,1)S(1)} %get-tuple-element.34.near_coef_ref, bf16[512,384]{1,0:T(8,128)(2,1)S(1)} %get-tuple-element.36.far_coef_ref, ...), custom_call_target="tpu_custom_call" | custom-call | flops 503316480 | bytes 1048576 | tf_op jit(solution)/shard_map/pallas_call | solution.py:48
  33.7 0.6 collective-permute-start.6
  34.3 0.1 collective-permute-done.7.got_ref
  34.3 0.1 shard_map.98
  34.4 1.6 %collective-permute-start.8 = (bf16[176,768]{1,0:T(8,128)(2,1)S(1)}, bf16[176,768]{1,0:T(8,128)(2,1)S(1)}, u32[]{:S(2)}, u32[]{:S(2)}) collective-permute-start(bf16[176,768]{1,0:T(8,128)(2,1)S(1)} %get-tuple-element.46), channel_id=1, source_target_pairs={{0,2},{1,3},{2,0},{3,1},{4,6},{5,7},{6,4},{7,5},{8,10},{9,11},{10,... | collective-permute-start | bytes 811016 | tf_op jit(solution)/shard_map/ppermute | solution.py:268
  36.0 0.9 %shard_map.97 = (f32[256,768]{1,0:T(8,128)S(1)}, bf16[128,768]{1,0:T(8,128)(2,1)S(1)}) custom-call(s32[1]{0:T(128)} %bitcast.base_ref, bf16[512,384]{1,0:T(8,128)(2,1)S(1)} %get-tuple-element.34.near_coef_ref, bf16[256,128]{1,0:T(8,128)(2,1)S(1)} %get-tuple-element.37.refs_0_, bf16[256,128]{1,0:T(8,128)(2,1)S(1)} %get-tuple-element.38.refs_1_, ...), custom_call_target="tpu_custom_call" | custom-call | flops 452984832 | bytes 1048576 | tf_op jit(solution)/shard_map/pallas_call | solution.py:48
  36.9 0.0 collective-permute-done.6.got_ref
  36.9 0.1 shard_map.99
  37.0 1.6 %collective-permute-start.10 = (bf16[160,768]{1,0:T(8,128)(2,1)S(1)}, bf16[160,768]{1,0:T(8,128)(2,1)S(1)}, u32[]{:S(2)}, u32[]{:S(2)}) collective-permute-start(bf16[160,768]{1,0:T(8,128)(2,1)S(1)} %get-tuple-element.49), channel_id=1, source_target_pairs={{0,16},{16,0},{1,17},{17,1},{2,18},{18,2},{3,19},{19,3},{4,20},{20... | collective-permute-start | bytes 737288 | tf_op jit(solution)/shard_map/ppermute | solution.py:271
  38.5 1.0 %collective-permute-start.12 = (bf16[128,768]{1,0:T(8,128)(2,1)S(1)}, bf16[128,768]{1,0:T(8,128)(2,1)S(1)}, u32[]{:S(2)}, u32[]{:S(2)}) collective-permute-start(bf16[128,768]{1,0:T(8,128)(2,1)S(1)} %get-tuple-element.57), channel_id=1, source_target_pairs={{0,4},{1,5},{2,6},{3,7},{4,0},{5,1},{6,2},{7,3},{8,12},{9,13},{10,... | collective-permute-start | bytes 589832 | tf_op jit(solution)/shard_map/ppermute | solution.py:268
  39.5 2.7 %collective-permute-start.13 = (bf16[128,768]{1,0:T(8,128)(2,1)S(1)}, bf16[128,768]{1,0:T(8,128)(2,1)S(1)}, u32[]{:S(2)}, u32[]{:S(2)}) collective-permute-start(bf16[128,768]{1,0:T(8,128)(2,1)S(1)} %get-tuple-element.58), channel_id=1, source_target_pairs={{0,8},{1,9},{2,10},{3,11},{4,12},{5,13},{6,14},{7,15},{8,0},{9,1},... | collective-permute-start | bytes 589832 | tf_op jit(solution)/shard_map/ppermute | solution.py:268
  42.2 0.3 collective-permute-start.14
  42.5 0.5 collective-permute-done.8.got_ref
  43.0 0.1 shard_map.100.mine_ref
  43.0 1.6 %collective-permute-start.9 = (bf16[176,768]{1,0:T(8,128)(2,1)S(1)}, bf16[176,768]{1,0:T(8,128)(2,1)S(1)}, u32[]{:S(2)}, u32[]{:S(2)}) collective-permute-start(bf16[176,768]{1,0:T(8,128)(2,1)S(1)} %shard_map.100.mine_ref), channel_id=1, source_target_pairs={{0,16},{16,0},{1,17},{17,1},{2,18},{18,2},{3,19},{19,3},{4,20},{20... | collective-permute-start | bytes 811016 | tf_op jit(solution)/shard_map/ppermute | solution.py:271
  44.6 0.1 collective-permute-done.10
  44.7 0.1 convert_add_fusion
  44.8 1.5 %collective-permute-start.11 = (bf16[80,768]{1,0:T(8,128)(2,1)S(1)}, bf16[80,768]{1,0:T(8,128)(2,1)S(1)}, u32[]{:S(2)}, u32[]{:S(2)}) collective-permute-start(bf16[80,768]{1,0:T(8,128)(2,1)S(1)} %slice.12), channel_id=1, source_target_pairs={{0,2},{1,3},{2,0},{3,1},{4,6},{5,7},{6,4},{7,5},{8,10},{9,11},{10,... | collective-permute-start | bytes 368648 | tf_op jit(solution)/shard_map/ppermute | solution.py:268
  46.3 0.4 collective-permute-done.12
  46.7 9.0 %collective-permute-done.13 = bf16[128,768]{1,0:T(8,128)(2,1)S(1)} collective-permute-done((bf16[128,768]{1,0:T(8,128)(2,1)S(1)}, bf16[128,768]{1,0:T(8,128)(2,1)S(1)}, u32[]{:S(2)}, u32[]{:S(2)}) %collective-permute-start.13) | collective-permute-done | bytes 196640 | tf_op jit(solution)/shard_map/ppermute | solution.py:268
  55.6 3.9 %collective-permute-done.14 = bf16[128,768]{1,0:T(8,128)(2,1)S(1)} collective-permute-done((bf16[128,768]{1,0:T(8,128)(2,1)S(1)}, bf16[128,768]{1,0:T(8,128)(2,1)S(1)}, u32[]{:S(2)}, u32[]{:S(2)}) %collective-permute-start.14) | collective-permute-done | bytes 196640 | tf_op jit(solution)/shard_map/ppermute | solution.py:268
  59.5 0.8 %add_convert_fusion = bf16[128,768]{1,0:T(8,128)(2,1)} fusion(bf16[128,768]{1,0:T(8,128)(2,1)S(1)} %collective-permute-done.14, bf16[128,768]{1,0:T(8,128)(2,1)S(1)} %collective-permute-done.13, f32[128,768]{1,0:T(8,128)S(1)} %get-tuple-element.56, bf16[128,768]{1,0:T(8,128)(2,1)S(1)} %collective-permute-done.12), kind=kLoop, calls=%fused_computation.1 | loop fusion | flops 688128 | bytes 1179648 | tf_op jit(solution)/shard_map/convert_element_type | solution.py:333
  60.3 0.0 collective-permute-done.11.got_ref
  60.3 1.0 %shard_map.101 = (bf16[256,768]{1,0:T(8,128)(2,1)}, f32[256,768]{1,0:T(8,128)}, f32[256,768]{1,0:T(8,128)}) custom-call(f32[80,768]{1,0:T(8,128)S(1)} %slice.9.mine_ref, bf16[80,768]{1,0:T(8,128)(2,1)S(1)} %collective-permute-done.11.got_ref, bf16[256,768]{1,0:T(8,128)(2,1)S(1)} %get-tuple-element.33.refs_3_.weights_ref, ...), custom_call_target="tpu_custom_call" | custom-call | flops 1228800 | bytes 1228800 | tf_op jit(solution)/shard_map/pallas_call | solution.py:244
  61.3 0.0 collective-permute-done.9.got_ref
  61.3 1.3 %shard_map.102 = (bf16[256,768]{1,0:T(8,128)(2,1)}, f32[256,768]{1,0:T(8,128)}, f32[256,768]{1,0:T(8,128)}) custom-call(bf16[176,768]{1,0:T(8,128)(2,1)S(1)} %shard_map.100.mine_ref, bf16[176,768]{1,0:T(8,128)(2,1)S(1)} %collective-permute-done.9.got_ref, ...), custom_call_target="tpu_custom_call", output_to_operand_aliasing={{0}: (5, {}), {1}: (6, {}), {2}: (7, {})} | custom-call | flops 2703360 | bytes 2703360 | tf_op jit(solution)/shard_map/pallas_call | solution.py:244
  (2 shorter events, 0.0 us)
Async XLA Ops:
  1.8 10.9 %collective-permute-start.3 = (bf16[256,768]{1,0:T(8,128)(2,1)S(1)}, bf16[256,768]{1,0:T(8,128)(2,1)S(1)}, u32[]{:S(2)}, u32[]{:S(2)}) collective-permute-start(bf16[256,768]{1,0:T(8,128)(2,1)S(1)} %get-tuple-element.33.refs_3_.weights_ref), channel_id=1, source_target_pairs={{0,2},{1,3},{2,0},{3,1},{4,6},{5,7},{6,4},{7,5},{8,10},{9,11},{10,... | collective-permute-start | bytes 1179656 | tf_op jit(solution)/shard_map/ppermute | solution.py:268
  3.4 22.8 %collective-permute-start.2 = (bf16[256,768]{1,0:T(8,128)(2,1)S(1)}, bf16[256,768]{1,0:T(8,128)(2,1)S(1)}, u32[]{:S(2)}, u32[]{:S(2)}) collective-permute-start(bf16[256,768]{1,0:T(8,128)(2,1)S(1)} %get-tuple-element.33.refs_3_.weights_ref), channel_id=1, source_target_pairs={{0,1},{1,0},{2,3},{3,2},{4,5},{5,4},{6,7},{7,6},{8,9},{9,8},{10,11... | collective-permute-start | bytes 1179656 | tf_op jit(solution)/shard_map/ppermute | solution.py:268
  12.7 14.9 %collective-permute-start.4 = (bf16[256,768]{1,0:T(8,128)(2,1)S(1)}, bf16[256,768]{1,0:T(8,128)(2,1)S(1)}, u32[]{:S(2)}, u32[]{:S(2)}) collective-permute-start(bf16[256,768]{1,0:T(8,128)(2,1)S(1)} %collective-permute-done.3.refs_3_.refs_1_.refs_5_), channel_id=1, source_target_pairs={{0,1},{1,0},{2,3},{3,2},{4,5},{5,4},{6,7},{7,6},{8,9},{9,8},{10,11... | collective-permute-start | bytes 1179656 | tf_op jit(solution)/shard_map/ppermute | solution.py:268
  12.7 12.1 %collective-permute-start.1 = (bf16[136,768]{1,0:T(8,128)(2,1)S(1)}, bf16[136,768]{1,0:T(8,128)(2,1)S(1)}, u32[]{:S(2)}, u32[]{:S(2)}) collective-permute-start(bf16[136,768]{1,0:T(8,128)(2,1)S(1)} %get-tuple-element.32.refs_0_.refs_2_.refs_7_), channel_id=1, source_target_pairs={{0,8},{1,9},{2,10},{3,11},{4,12},{5,13},{6,14},{7,15},{8,0},{9,1},... | collective-permute-start | bytes 626696 | tf_op jit(solution)/shard_map/ppermute | solution.py:268
  15.3 10.9 %collective-permute-start = (bf16[136,768]{1,0:T(8,128)(2,1)S(1)}, bf16[136,768]{1,0:T(8,128)(2,1)S(1)}, u32[]{:S(2)}, u32[]{:S(2)}) collective-permute-start(bf16[136,768]{1,0:T(8,128)(2,1)S(1)} %get-tuple-element.32.refs_0_.refs_2_.refs_7_), channel_id=1, source_target_pairs={{0,4},{1,5},{2,6},{3,7},{4,0},{5,1},{6,2},{7,3},{8,12},{9,13},{10,... | collective-permute-start | bytes 626696 | tf_op jit(solution)/shard_map/ppermute | solution.py:268
  24.8 7.1 %collective-permute-start.5 = (bf16[136,768]{1,0:T(8,128)(2,1)S(1)}, bf16[136,768]{1,0:T(8,128)(2,1)S(1)}, u32[]{:S(2)}, u32[]{:S(2)}) collective-permute-start(bf16[136,768]{1,0:T(8,128)(2,1)S(1)} %collective-permute-done.1.refs_2_.refs_4_.refs_9_), channel_id=1, source_target_pairs={{0,4},{1,5},{2,6},{3,7},{4,0},{5,1},{6,2},{7,3},{8,12},{9,13},{10,... | collective-permute-start | bytes 626696 | tf_op jit(solution)/shard_map/ppermute | solution.py:268
  32.5 1.8 %collective-permute-start.7 = (bf16[256,768]{1,0:T(8,128)(2,1)S(1)}, bf16[256,768]{1,0:T(8,128)(2,1)S(1)}, u32[]{:S(2)}, u32[]{:S(2)}) collective-permute-start(bf16[256,768]{1,0:T(8,128)(2,1)S(1)} %get-tuple-element.43), channel_id=1, source_target_pairs={{0,1},{1,0},{2,3},{3,2},{4,5},{5,4},{6,7},{7,6},{8,9},{9,8},{10,11... | collective-permute-start | bytes 1179656 | tf_op jit(solution)/shard_map/ppermute | solution.py:268
  33.7 3.2 %collective-permute-start.6 = (bf16[256,768]{1,0:T(8,128)(2,1)S(1)}, bf16[256,768]{1,0:T(8,128)(2,1)S(1)}, u32[]{:S(2)}, u32[]{:S(2)}) collective-permute-start(bf16[256,768]{1,0:T(8,128)(2,1)S(1)} %get-tuple-element.41), channel_id=1, source_target_pairs={{0,1},{1,0},{2,3},{3,2},{4,5},{5,4},{6,7},{7,6},{8,9},{9,8},{10,11... | collective-permute-start | bytes 1179656 | tf_op jit(solution)/shard_map/ppermute | solution.py:268
  34.4 8.6 %collective-permute-start.8 = (bf16[176,768]{1,0:T(8,128)(2,1)S(1)}, bf16[176,768]{1,0:T(8,128)(2,1)S(1)}, u32[]{:S(2)}, u32[]{:S(2)}) collective-permute-start(bf16[176,768]{1,0:T(8,128)(2,1)S(1)} %get-tuple-element.46), channel_id=1, source_target_pairs={{0,2},{1,3},{2,0},{3,1},{4,6},{5,7},{6,4},{7,5},{8,10},{9,11},{10,... | collective-permute-start | bytes 811016 | tf_op jit(solution)/shard_map/ppermute | solution.py:268
  37.0 7.8 %collective-permute-start.10 = (bf16[160,768]{1,0:T(8,128)(2,1)S(1)}, bf16[160,768]{1,0:T(8,128)(2,1)S(1)}, u32[]{:S(2)}, u32[]{:S(2)}) collective-permute-start(bf16[160,768]{1,0:T(8,128)(2,1)S(1)} %get-tuple-element.49), channel_id=1, source_target_pairs={{0,16},{16,0},{1,17},{17,1},{2,18},{18,2},{3,19},{19,3},{4,20},{20... | collective-permute-start | bytes 737288 | tf_op jit(solution)/shard_map/ppermute | solution.py:271
  38.5 8.2 %collective-permute-start.12 = (bf16[128,768]{1,0:T(8,128)(2,1)S(1)}, bf16[128,768]{1,0:T(8,128)(2,1)S(1)}, u32[]{:S(2)}, u32[]{:S(2)}) collective-permute-start(bf16[128,768]{1,0:T(8,128)(2,1)S(1)} %get-tuple-element.57), channel_id=1, source_target_pairs={{0,4},{1,5},{2,6},{3,7},{4,0},{5,1},{6,2},{7,3},{8,12},{9,13},{10,... | collective-permute-start | bytes 589832 | tf_op jit(solution)/shard_map/ppermute | solution.py:268
  39.5 16.2 %collective-permute-start.13 = (bf16[128,768]{1,0:T(8,128)(2,1)S(1)}, bf16[128,768]{1,0:T(8,128)(2,1)S(1)}, u32[]{:S(2)}, u32[]{:S(2)}) collective-permute-start(bf16[128,768]{1,0:T(8,128)(2,1)S(1)} %get-tuple-element.58), channel_id=1, source_target_pairs={{0,8},{1,9},{2,10},{3,11},{4,12},{5,13},{6,14},{7,15},{8,0},{9,1},... | collective-permute-start | bytes 589832 | tf_op jit(solution)/shard_map/ppermute | solution.py:268
  42.2 17.3 %collective-permute-start.14 = (bf16[128,768]{1,0:T(8,128)(2,1)S(1)}, bf16[128,768]{1,0:T(8,128)(2,1)S(1)}, u32[]{:S(2)}, u32[]{:S(2)}) collective-permute-start(bf16[128,768]{1,0:T(8,128)(2,1)S(1)} %get-tuple-element.59), channel_id=1, source_target_pairs={{0,12},{1,13},{2,14},{3,15},{4,8},{5,9},{6,10},{7,11},{8,4},{9,5},... | collective-permute-start | bytes 589832 | tf_op jit(solution)/shard_map/ppermute | solution.py:268
  43.0 18.3 %collective-permute-start.9 = (bf16[176,768]{1,0:T(8,128)(2,1)S(1)}, bf16[176,768]{1,0:T(8,128)(2,1)S(1)}, u32[]{:S(2)}, u32[]{:S(2)}) collective-permute-start(bf16[176,768]{1,0:T(8,128)(2,1)S(1)} %shard_map.100.mine_ref), channel_id=1, source_target_pairs={{0,16},{16,0},{1,17},{17,1},{2,18},{18,2},{3,19},{19,3},{4,20},{20... | collective-permute-start | bytes 811016 | tf_op jit(solution)/shard_map/ppermute | solution.py:271
  44.8 15.5 %collective-permute-start.11 = (bf16[80,768]{1,0:T(8,128)(2,1)S(1)}, bf16[80,768]{1,0:T(8,128)(2,1)S(1)}, u32[]{:S(2)}, u32[]{:S(2)}) collective-permute-start(bf16[80,768]{1,0:T(8,128)(2,1)S(1)} %slice.12), channel_id=1, source_target_pairs={{0,2},{1,3},{2,0},{3,1},{4,6},{5,7},{6,4},{7,5},{8,10},{9,11},{10,... | collective-permute-start | bytes 368648 | tf_op jit(solution)/shard_map/ppermute | solution.py:268

commit v3 on v2

--- a/solution.py
+++ b/solution.py
@@ -179,14 +179,17 @@
     )
 
 
-def last_kernel(rows, labels, base_ref, near_coef_ref, *refs):
-    coef_refs, weight_refs = refs[: NEAR - 1], refs[NEAR - 1 : 2 * NEAR - 1]
-    packed_refs, (own_ref, back_ref) = refs[2 * NEAR - 1 : 3 * NEAR - 1], refs[3 * NEAR - 1 :]
-    coef, own_ref[...] = grad_part(
-        rows, 0, base_ref, weight_refs[0], near_coef_ref[:labels, :], packed_refs
-    )
-    total = tn_dot(coef, weight_refs[0][...])
-    for coef_ref, weight_ref in zip(coef_refs, weight_refs[1:]):
+def last_kernel(rows, labels, base_ref, near_coef_ref, weight_ref, *refs):
+    packed_refs, (coef_ref, own_ref) = refs[:NEAR], refs[NEAR:]
+    coef_ref[...], own_ref[...] = grad_part(
+        rows, 0, base_ref, weight_ref, near_coef_ref[:labels, :], packed_refs
+    )
+
+
+def back_kernel(rows, labels, base_ref, *refs):
+    coef_refs, weight_refs, back_ref = refs[:NEAR], refs[NEAR : 2 * NEAR], refs[-1]
+    total = jnp.zeros(back_ref.shape, jnp.float32)
+    for coef_ref, weight_ref in zip(coef_refs, weight_refs):
         total = total + tn_dot(coef_ref[...], weight_ref[...])
     back_ref[...] = total.astype(back_ref.dtype)
 
@@ -212,8 +215,7 @@
 
 
 def adam_kernel(start, pieces, mine_ref, got_ref, weights_ref, first_ref, second_ref, *refs):
-    *outs, sems = refs[-7:]
-    outs_hbm, scratch = outs[:3], outs[3:]
+    outs_hbm, scratch, sems = refs[-7:-4], refs[-4:-1], refs[-1]
     copies, at = [], 0
     for piece, rows in enumerate(pieces):
         here, there = slice(at, at + rows), slice(start + at, start + at + rows)
@@ -236,24 +238,49 @@
         copy.wait()
 
 
-def adam_work(start, mine, got, old, earlier):
+def end_kernel(pieces, mine_ref, got_ref, weights_ref, first_ref, second_ref, total_ref, *refs):
+    back_refs, refs = refs[: NEAR - 1], refs[NEAR - 1 :]
+    _, _, _, *outs, query_hbm = refs[:7]
+    *scratch, sems, query_ref, query_sem = refs[7:]
+    total = total_ref[...]
+    for ref in back_refs:
+        total = total + ref[...].astype(jnp.float32)
+    query_ref[...] = total.astype(query_ref.dtype)
+    copy = pltpu.make_async_copy(query_ref, query_hbm, query_sem.at[0])
+    copy.start()
+    adam_kernel(
+        0, pieces, mine_ref, got_ref, weights_ref, first_ref, second_ref, *outs, *scratch, sems
+    )
+    copy.wait()
+
+
+def adam_work(start, mine, got, old, earlier, queries=()):
     rows, dim = mine.shape
     pieces = [min(PIECE, rows - at) for at in range(0, rows, PIECE)]
     vmem, hbm = pl.BlockSpec(memory_space=pltpu.VMEM), pl.BlockSpec(memory_space=pltpu.HBM)
     earlier = [pltpu.with_memory_space_constraint(x, pltpu.HBM) for x in earlier]
+    outs = [pltpu.HBM(x.shape, x.dtype) for x in old]
+    scratch = [pltpu.VMEM((rows, dim), x.dtype) for x in old]
+    scratch.append(pltpu.SemaphoreType.DMA((3, len(pieces))))
+    body = functools.partial(adam_kernel, start, pieces)
+    if queries:
+        shape, kind = queries[0].shape, queries[1].dtype
+        outs.append(pltpu.HBM(shape, kind))
+        scratch += [pltpu.VMEM(shape, kind), pltpu.SemaphoreType.DMA((1,))]
+        body = functools.partial(end_kernel, pieces)
+    ahead = 5 + len(queries)
     return pl.pallas_call(
-        functools.partial(adam_kernel, start, pieces),
-        out_shape=tuple(pltpu.HBM(x.shape, x.dtype) for x in old),
-        in_specs=[vmem] * 5 + [hbm] * len(earlier),
-        out_specs=(hbm, hbm, hbm),
-        scratch_shapes=[pltpu.VMEM((rows, dim), x.dtype) for x in old]
-        + [pltpu.SemaphoreType.DMA((3, len(pieces)))],
-        input_output_aliases={5 + i: i for i in range(len(earlier))},
+        body,
+        out_shape=tuple(outs),
+        in_specs=[vmem] * ahead + [hbm] * len(earlier),
+        out_specs=tuple([hbm] * len(outs)),
+        scratch_shapes=scratch,
+        input_output_aliases={ahead + i: i for i in range(len(earlier))},
         compiler_params=pltpu.CompilerParams(vmem_limit_bytes=KERNEL_VMEM),
         cost_estimate=pl.CostEstimate(
             flops=20 * rows * dim, bytes_accessed=20 * rows * dim, transcendentals=rows * dim
         ),
-    )(mine, got, *old, *earlier)
+    )(mine, got, *old, *queries, *earlier)
 
 
 def near_device(queries, shortlist, positives, weights, first_moment, second_moment):
@@ -314,12 +341,10 @@
         labels * dim,
     )
     got_top = over_cluster(top_near, 2)
-    own, back = kernel(
-        last_kernel,
-        [((labels, dim), wide), block],
-        [near_coef, coef1, coef2, coef3, *near_weights, *packs],
-        9,
-    )
+    coef0, own = kernel(
+        last_kernel, [last_coef, ((labels, dim), wide)], [near_coef, near_weights[0], *packs], 5
+    )
+    (back,) = kernel(back_kernel, [block], [coef0, coef1, coef2, coef3, *near_weights], 4)
     backs.append(back)
     own_top, low = kernel_call(
         mine_kernel,
@@ -328,9 +353,7 @@
         labels * dim,
     )
     got_low = over_dp(low).astype(wide)
-    for s, back in enumerate(backs, 1):
-        total = total + over_cluster(back, s * NEAR).astype(wide)
-    query_grad = total.astype(low_type)
+    returned = [over_cluster(back, s * NEAR) for s, back in enumerate(backs, 1)]
 
     (top,) = kernel_call(sum_kernel, [((cut, dim), low_type)], [base, own_top, got_top], cut * dim)
     low = low.astype(wide) + got_low
@@ -338,7 +361,9 @@
     got_top, got_low = over_dp(top), over_cluster(low_near, 2)
     old = (own_weights, old_first, old_second)
     partly = adam_work(cut, low_own, got_low, old, ())
-    new_weights, new_first, new_second = adam_work(0, top, got_top, old, partly)
+    new_weights, new_first, new_second, query_grad = adam_work(
+        0, top, got_top, old, partly, (total, *returned)
+    )
     return (new_weights[None], new_first[None], new_second[None], query_grad)
 
 

time: 62.8 us -> 62.2 us (level)
  the two profiles are of different devices: /device:TPU:8 before, /device:TPU:0 now
where the time goes in v3:
time: 62.2 us; the launch traced here: 62.1 us
  waiting for transfers between devices  32.9 us (53%)
  starting transfers between devices  19.2 us (31%)
  Pallas kernels  9.18 us (15%)
  between operations  0.76 us (1%)
    ppermute x13, waiting for transfers between devices, over_cluster(): return lax.ppermute(x, 'cluster', [(i, i ^ bits) for i in range(owners)])  32.9 us
    ppermute x13, starting transfers between devices, over_cluster(): return lax.ppermute(x, 'cluster', [(i, i ^ bits) for i in range(owners)])  16.3 us
    pallas_call x9, Pallas kernels, kernel_call(): pl.pallas_call(kernel, out_shape=tuple((jax.ShapeDtypeStruct(shape, kind)...  5.63 us
    ppermute x2, starting transfers between devices, over_dp(): return lax.ppermute(x, 'dp', [(0, 1), (1, 0)])  2.84 us
    pallas_call x2, Pallas kernels, adam_work(): pl.pallas_call(body, out_shape=tuple(outs), in_specs=[vmem] * ahead + [hb...  2.37 us
  transfers between devices with their start and end apart: 15, of which 7 were waited for; matrix products, arithmetic and copies ran while one was open for 0% of the time, Pallas kernels for 10%

profile of v3, /device:TPU:0, one launch (start us, length us, event | category | flops | bytes accessed | tf_op | source)
XLA Modules:
  0.0 62.1 jit_solution(16128520674204285826)
XLA Ops:
  0.6 1.2 %load.1 = (bf16[136,768]{1,0:T(8,128)(2,1)S(1)}, bf16[256,768]{1,0:T(8,128)(2,1)S(1)}) custom-call(bf16[128,768]{1,0:T(8,128)(2,1)} %q_hbm.1, s32[8,128]{1,0:T(8,128)} %bitcast.15, s32[8,128]{1,0:T(8,128)} %bitcast.16, bf16[256,768]{1,0:T(8,128)(2,1)} %bitcast.13), custom_call_target="tpu_custom_call" | custom-call | tf_op jit(solution)/shard_map/load/pallas_call | solution.py:101
  1.8 3.1 %collective-permute-start.4 = (bf16[256,768]{1,0:T(8,128)(2,1)S(1)}, bf16[256,768]{1,0:T(8,128)(2,1)S(1)}, u32[]{:S(2)}, u32[]{:S(2)}) collective-permute-start(bf16[256,768]{1,0:T(8,128)(2,1)S(1)} %get-tuple-element.34.refs_3_.weight_ref.refs_4_.weights_ref), channel_id=1, source_target_pairs={{0,2},{1,3},{2,0},{3,1},{4,6},{5,7},{6,4},{7,5},{8,10},{9,11},{10,... | collective-permute-start | bytes 1179656 | tf_op jit(solution)/shard_map/ppermute | solution.py:295
  4.9 0.0 collective-permute-start.2
  4.9 9.1 %collective-permute-done.4.refs_3_.refs_1_.refs_6_ = bf16[256,768]{1,0:T(8,128)(2,1)S(1)} collective-permute-done((bf16[256,768]{1,0:T(8,128)(2,1)S(1)}, bf16[256,768]{1,0:T(8,128)(2,1)S(1)}, u32[]{:S(2)}, u32[]{:S(2)}) %collective-permute-start.4) | collective-permute-done | bytes 393248 | tf_op jit(solution)/shard_map/ppermute | solution.py:295
  14.0 0.0 collective-permute-start.5
  14.0 2.8 %collective-permute-start.1 = (bf16[136,768]{1,0:T(8,128)(2,1)S(1)}, bf16[136,768]{1,0:T(8,128)(2,1)S(1)}, u32[]{:S(2)}, u32[]{:S(2)}) collective-permute-start(bf16[136,768]{1,0:T(8,128)(2,1)S(1)} %get-tuple-element.33.refs_0_.refs_2_), channel_id=1, source_target_pairs={{0,8},{1,9},{2,10},{3,11},{4,12},{5,13},{6,14},{7,15},{8,0},{9,1},... | collective-permute-start | bytes 626696 | tf_op jit(solution)/shard_map/ppermute | solution.py:295
  16.8 1.6 %collective-permute-start = (bf16[136,768]{1,0:T(8,128)(2,1)S(1)}, bf16[136,768]{1,0:T(8,128)(2,1)S(1)}, u32[]{:S(2)}, u32[]{:S(2)}) collective-permute-start(bf16[136,768]{1,0:T(8,128)(2,1)S(1)} %get-tuple-element.33.refs_0_.refs_2_), channel_id=1, source_target_pairs={{0,4},{1,5},{2,6},{3,7},{4,0},{5,1},{6,2},{7,3},{8,12},{9,13},{10,... | collective-permute-start | bytes 626696 | tf_op jit(solution)/shard_map/ppermute | solution.py:295
  18.4 8.8 %collective-permute-done.1.refs_2_.refs_4_ = bf16[136,768]{1,0:T(8,128)(2,1)S(1)} collective-permute-done((bf16[136,768]{1,0:T(8,128)(2,1)S(1)}, bf16[136,768]{1,0:T(8,128)(2,1)S(1)}, u32[]{:S(2)}, u32[]{:S(2)}) %collective-permute-start.1) | collective-permute-done | bytes 208928 | tf_op jit(solution)/shard_map/ppermute | solution.py:295
  27.2 0.6 %collective-permute-start.3 = (bf16[136,768]{1,0:T(8,128)(2,1)S(1)}, bf16[136,768]{1,0:T(8,128)(2,1)S(1)}, u32[]{:S(2)}, u32[]{:S(2)}) collective-permute-start(bf16[136,768]{1,0:T(8,128)(2,1)S(1)} %collective-permute-done.1.refs_2_.refs_4_), channel_id=1, source_target_pairs={{0,4},{1,5},{2,6},{3,7},{4,0},{5,1},{6,2},{7,3},{8,12},{9,13},{10,... | collective-permute-start | bytes 626696 | tf_op jit(solution)/shard_map/ppermute | solution.py:295
  27.9 0.0 collective-permute-done.refs_1_.refs_3_
  27.9 0.0 collective-permute-done.2.refs_4_.refs_0_.refs_5_
  27.9 1.4 %shard_map.93 = (bf16[512,384]{1,0:T(8,128)(2,1)S(1)}, f32[384,768]{1,0:T(8,128)S(1)}, f32[256,768]{1,0:T(8,128)S(1)}, f32[256,768]{1,0:T(8,128)S(1)}) custom-call(s32[1]{0:T(128)} %bitcast.base_ref, f32[256,768]{1,0:T(8,128)} %bitcast.9, f32[256,768]{1,0:T(8,128)} %bitcast.10, bf16[136,768]{1,0:T(8,128)(2,1)S(1)} %get-tuple-element.33.refs_0_.refs_2_, ...), custom_call_target="tpu_custom_call" | custom-call | flops 603979776 | bytes 1048576 | tf_op jit(solution)/shard_map/pallas_call | solution.py:48
  29.3 0.0 collective-permute-done.5.refs_4_.weight_ref.refs_7_
  29.3 1.3 %shard_map.95 = (bf16[512,384]{1,0:T(8,128)(2,1)S(1)}, f32[128,768]{1,0:T(8,128)S(1)}, bf16[128,768]{1,0:T(8,128)(2,1)S(1)}, bf16[128,768]{1,0:T(8,128)(2,1)S(1)}) custom-call(s32[1]{0:T(128)} %bitcast.base_ref, bf16[136,768]{1,0:T(8,128)(2,1)S(1)} %get-tuple-element.33.refs_0_.refs_2_, bf16[136,768]{1,0:T(8,128)(2,1)S(1)} %collective-permute-done.refs_1_.refs_3_, ...), custom_call_target="tpu_custom_call" | custom-call | flops 603979776 | bytes 1048576 | tf_op jit(solution)/shard_map/pallas_call | solution.py:48
  30.6 3.4 %collective-permute-done.3.refs_3_.refs_5_ = bf16[136,768]{1,0:T(8,128)(2,1)S(1)} collective-permute-done((bf16[136,768]{1,0:T(8,128)(2,1)S(1)}, bf16[136,768]{1,0:T(8,128)(2,1)S(1)}, u32[]{:S(2)}, u32[]{:S(2)}) %collective-permute-start.3) | collective-permute-done | bytes 208928 | tf_op jit(solution)/shard_map/ppermute | solution.py:295
  34.0 0.6 shard_map.97
  34.6 0.1 collective-permute-start.7
  34.7 1.1 %shard_map.96 = (bf16[256,128]{1,0:T(8,128)(2,1)S(1)}, bf16[256,128]{1,0:T(8,128)(2,1)S(1)}, bf16[256,768]{1,0:T(8,128)(2,1)S(1)}, f32[256,768]{1,0:T(8,128)S(1)}) custom-call(s32[1]{0:T(128)} %bitcast.base_ref, bf16[512,384]{1,0:T(8,128)(2,1)S(1)} %get-tuple-element.35.near_coef_ref, bf16[512,384]{1,0:T(8,128)(2,1)S(1)} %get-tuple-element.38.far_coef_ref, ...), custom_call_target="tpu_custom_call" | custom-call | flops 503316480 | bytes 1048576 | tf_op jit(solution)/shard_map/pallas_call | solution.py:48
  35.8 0.6 collective-permute-start.6
  36.4 0.1 collective-permute-done.7.got_ref
  36.4 0.1 shard_map.98
  36.5 1.5 %collective-permute-start.8 = (bf16[176,768]{1,0:T(8,128)(2,1)S(1)}, bf16[176,768]{1,0:T(8,128)(2,1)S(1)}, u32[]{:S(2)}, u32[]{:S(2)}) collective-permute-start(bf16[176,768]{1,0:T(8,128)(2,1)S(1)} %get-tuple-element.44), channel_id=1, source_target_pairs={{0,2},{1,3},{2,0},{3,1},{4,6},{5,7},{6,4},{7,5},{8,10},{9,11},{10,... | collective-permute-start | bytes 811016 | tf_op jit(solution)/shard_map/ppermute | solution.py:295
  38.0 0.6 shard_map.94
  38.6 0.0 collective-permute-done.6.got_ref
  38.6 0.1 shard_map.99
  38.7 1.6 %collective-permute-start.13 = (bf16[160,768]{1,0:T(8,128)(2,1)S(1)}, bf16[160,768]{1,0:T(8,128)(2,1)S(1)}, u32[]{:S(2)}, u32[]{:S(2)}) collective-permute-start(bf16[160,768]{1,0:T(8,128)(2,1)S(1)} %get-tuple-element.54), channel_id=1, source_target_pairs={{0,16},{16,0},{1,17},{17,1},{2,18},{18,2},{3,19},{19,3},{4,20},{20... | collective-permute-start | bytes 737288 | tf_op jit(solution)/shard_map/ppermute | solution.py:298
  40.2 0.4 shard_map.101
  40.7 3.9 %collective-permute-start.12 = (bf16[128,768]{1,0:T(8,128)(2,1)S(1)}, bf16[128,768]{1,0:T(8,128)(2,1)S(1)}, u32[]{:S(2)}, u32[]{:S(2)}) collective-permute-start(bf16[128,768]{1,0:T(8,128)(2,1)S(1)} %shard_map.101), channel_id=1, source_target_pairs={{0,12},{1,13},{2,14},{3,15},{4,8},{5,9},{6,10},{7,11},{8,4},{9,5},... | collective-permute-start | bytes 589832 | tf_op jit(solution)/shard_map/ppermute | solution.py:295
  44.6 0.0 collective-permute-start.10
  44.6 0.6 %collective-permute-start.11 = (bf16[128,768]{1,0:T(8,128)(2,1)S(1)}, bf16[128,768]{1,0:T(8,128)(2,1)S(1)}, u32[]{:S(2)}, u32[]{:S(2)}) collective-permute-start(bf16[128,768]{1,0:T(8,128)(2,1)S(1)} %get-tuple-element.49), channel_id=1, source_target_pairs={{0,8},{1,9},{2,10},{3,11},{4,12},{5,13},{6,14},{7,15},{8,0},{9,1},... | collective-permute-start | bytes 589832 | tf_op jit(solution)/shard_map/ppermute | solution.py:295
  45.2 0.0 collective-permute-done.8.got_ref
  45.3 1.3 %collective-permute-start.9 = (bf16[176,768]{1,0:T(8,128)(2,1)S(1)}, bf16[176,768]{1,0:T(8,128)(2,1)S(1)}, u32[]{:S(2)}, u32[]{:S(2)}) collective-permute-start(bf16[176,768]{1,0:T(8,128)(2,1)S(1)} %shard_map.100.mine_ref), channel_id=1, source_target_pairs={{0,16},{16,0},{1,17},{17,1},{2,18},{18,2},{3,19},{19,3},{4,20},{20... | collective-permute-start | bytes 811016 | tf_op jit(solution)/shard_map/ppermute | solution.py:298
  46.6 0.0 collective-permute-done.13
  46.6 0.1 convert_add_fusion
  46.7 1.6 %collective-permute-start.14 = (bf16[80,768]{1,0:T(8,128)(2,1)S(1)}, bf16[80,768]{1,0:T(8,128)(2,1)S(1)}, u32[]{:S(2)}, u32[]{:S(2)}) collective-permute-start(bf16[80,768]{1,0:T(8,128)(2,1)S(1)} %slice.12), channel_id=1, source_target_pairs={{0,2},{1,3},{2,0},{3,1},{4,6},{5,7},{6,4},{7,5},{8,10},{9,11},{10,... | collective-permute-start | bytes 368648 | tf_op jit(solution)/shard_map/ppermute | solution.py:295
  48.3 3.3 %collective-permute-done.14.got_ref = bf16[80,768]{1,0:T(8,128)(2,1)S(1)} collective-permute-done((bf16[80,768]{1,0:T(8,128)(2,1)S(1)}, bf16[80,768]{1,0:T(8,128)(2,1)S(1)}, u32[]{:S(2)}, u32[]{:S(2)}) %collective-permute-start.14) | collective-permute-done | bytes 122912 | tf_op jit(solution)/shard_map/ppermute | solution.py:295
  51.6 1.0 %shard_map.102 = (bf16[256,768]{1,0:T(8,128)(2,1)}, f32[256,768]{1,0:T(8,128)}, f32[256,768]{1,0:T(8,128)}) custom-call(f32[80,768]{1,0:T(8,128)S(1)} %slice.9.mine_ref, bf16[80,768]{1,0:T(8,128)(2,1)S(1)} %collective-permute-done.14.got_ref, bf16[256,768]{1,0:T(8,128)(2,1)S(1)} %get-tuple-element.34.refs_3_.weight_ref.refs_4_.weights_ref, ...), custom_call_target="tpu_custom_call" | custom-call | flops 1228800 | bytes 1228800 | tf_op jit(solution)/shard_map/pallas_call | solution.py:272
  52.6 0.0 collective-permute-done.12.refs_2_
  52.6 2.2 %collective-permute-done.10.refs_0_ = bf16[128,768]{1,0:T(8,128)(2,1)S(1)} collective-permute-done((bf16[128,768]{1,0:T(8,128)(2,1)S(1)}, bf16[128,768]{1,0:T(8,128)(2,1)S(1)}, u32[]{:S(2)}, u32[]{:S(2)}) %collective-permute-start.10) | collective-permute-done | bytes 196640 | tf_op jit(solution)/shard_map/ppermute | solution.py:295
  54.9 5.8 %collective-permute-done.11.refs_1_ = bf16[128,768]{1,0:T(8,128)(2,1)S(1)} collective-permute-done((bf16[128,768]{1,0:T(8,128)(2,1)S(1)}, bf16[128,768]{1,0:T(8,128)(2,1)S(1)}, u32[]{:S(2)}, u32[]{:S(2)}) %collective-permute-start.11) | collective-permute-done | bytes 196640 | tf_op jit(solution)/shard_map/ppermute | solution.py:295
  60.7 0.0 collective-permute-done.9.got_ref
  60.7 1.4 %shard_map.103 = (bf16[256,768]{1,0:T(8,128)(2,1)}, f32[256,768]{1,0:T(8,128)}, f32[256,768]{1,0:T(8,128)}, bf16[128,768]{1,0:T(8,128)(2,1)}) custom-call(bf16[176,768]{1,0:T(8,128)(2,1)S(1)} %shard_map.100.mine_ref, bf16[176,768]{1,0:T(8,128)(2,1)S(1)} %collective-permute-done.9.got_ref, ...), custom_call_target="tpu_custom_call", output_to_operand_aliasing={{0}: (9, {}), {1}: (10, {}), {2}: (11, {})} | custom-call | flops 2703360 | bytes 2703360 | tf_op jit(solution)/shard_map/pallas_call | solution.py:272
  (3 shorter events, 0.1 us)
Async XLA Ops:
  1.8 12.2 %collective-permute-start.4 = (bf16[256,768]{1,0:T(8,128)(2,1)S(1)}, bf16[256,768]{1,0:T(8,128)(2,1)S(1)}, u32[]{:S(2)}, u32[]{:S(2)}) collective-permute-start(bf16[256,768]{1,0:T(8,128)(2,1)S(1)} %get-tuple-element.34.refs_3_.weight_ref.refs_4_.weights_ref), channel_id=1, source_target_pairs={{0,2},{1,3},{2,0},{3,1},{4,6},{5,7},{6,4},{7,5},{8,10},{9,11},{10,... | collective-permute-start | bytes 1179656 | tf_op jit(solution)/shard_map/ppermute | solution.py:295
  4.9 23.0 %collective-permute-start.2 = (bf16[256,768]{1,0:T(8,128)(2,1)S(1)}, bf16[256,768]{1,0:T(8,128)(2,1)S(1)}, u32[]{:S(2)}, u32[]{:S(2)}) collective-permute-start(bf16[256,768]{1,0:T(8,128)(2,1)S(1)} %get-tuple-element.34.refs_3_.weight_ref.refs_4_.weights_ref), channel_id=1, source_target_pairs={{0,1},{1,0},{2,3},{3,2},{4,5},{5,4},{6,7},{7,6},{8,9},{9,8},{10,11... | collective-permute-start | bytes 1179656 | tf_op jit(solution)/shard_map/ppermute | solution.py:295
  14.0 15.3 %collective-permute-start.5 = (bf16[256,768]{1,0:T(8,128)(2,1)S(1)}, bf16[256,768]{1,0:T(8,128)(2,1)S(1)}, u32[]{:S(2)}, u32[]{:S(2)}) collective-permute-start(bf16[256,768]{1,0:T(8,128)(2,1)S(1)} %collective-permute-done.4.refs_3_.refs_1_.refs_6_), channel_id=1, source_target_pairs={{0,1},{1,0},{2,3},{3,2},{4,5},{5,4},{6,7},{7,6},{8,9},{9,8},{10,11... | collective-permute-start | bytes 1179656 | tf_op jit(solution)/shard_map/ppermute | solution.py:295
  14.0 13.2 %collective-permute-start.1 = (bf16[136,768]{1,0:T(8,128)(2,1)S(1)}, bf16[136,768]{1,0:T(8,128)(2,1)S(1)}, u32[]{:S(2)}, u32[]{:S(2)}) collective-permute-start(bf16[136,768]{1,0:T(8,128)(2,1)S(1)} %get-tuple-element.33.refs_0_.refs_2_), channel_id=1, source_target_pairs={{0,8},{1,9},{2,10},{3,11},{4,12},{5,13},{6,14},{7,15},{8,0},{9,1},... | collective-permute-start | bytes 626696 | tf_op jit(solution)/shard_map/ppermute | solution.py:295
  16.8 11.1 %collective-permute-start = (bf16[136,768]{1,0:T(8,128)(2,1)S(1)}, bf16[136,768]{1,0:T(8,128)(2,1)S(1)}, u32[]{:S(2)}, u32[]{:S(2)}) collective-permute-start(bf16[136,768]{1,0:T(8,128)(2,1)S(1)} %get-tuple-element.33.refs_0_.refs_2_), channel_id=1, source_target_pairs={{0,4},{1,5},{2,6},{3,7},{4,0},{5,1},{6,2},{7,3},{8,12},{9,13},{10,... | collective-permute-start | bytes 626696 | tf_op jit(solution)/shard_map/ppermute | solution.py:295
  27.2 6.8 %collective-permute-start.3 = (bf16[136,768]{1,0:T(8,128)(2,1)S(1)}, bf16[136,768]{1,0:T(8,128)(2,1)S(1)}, u32[]{:S(2)}, u32[]{:S(2)}) collective-permute-start(bf16[136,768]{1,0:T(8,128)(2,1)S(1)} %collective-permute-done.1.refs_2_.refs_4_), channel_id=1, source_target_pairs={{0,4},{1,5},{2,6},{3,7},{4,0},{5,1},{6,2},{7,3},{8,12},{9,13},{10,... | collective-permute-start | bytes 626696 | tf_op jit(solution)/shard_map/ppermute | solution.py:295
  34.6 1.8 %collective-permute-start.7 = (bf16[256,768]{1,0:T(8,128)(2,1)S(1)}, bf16[256,768]{1,0:T(8,128)(2,1)S(1)}, u32[]{:S(2)}, u32[]{:S(2)}) collective-permute-start(bf16[256,768]{1,0:T(8,128)(2,1)S(1)} %get-tuple-element.41), channel_id=1, source_target_pairs={{0,1},{1,0},{2,3},{3,2},{4,5},{5,4},{6,7},{7,6},{8,9},{9,8},{10,11... | collective-permute-start | bytes 1179656 | tf_op jit(solution)/shard_map/ppermute | solution.py:295
  35.8 2.7 %collective-permute-start.6 = (bf16[256,768]{1,0:T(8,128)(2,1)S(1)}, bf16[256,768]{1,0:T(8,128)(2,1)S(1)}, u32[]{:S(2)}, u32[]{:S(2)}) collective-permute-start(bf16[256,768]{1,0:T(8,128)(2,1)S(1)} %get-tuple-element.39), channel_id=1, source_target_pairs={{0,1},{1,0},{2,3},{3,2},{4,5},{5,4},{6,7},{7,6},{8,9},{9,8},{10,11... | collective-permute-start | bytes 1179656 | tf_op jit(solution)/shard_map/ppermute | solution.py:295
  36.5 8.7 %collective-permute-start.8 = (bf16[176,768]{1,0:T(8,128)(2,1)S(1)}, bf16[176,768]{1,0:T(8,128)(2,1)S(1)}, u32[]{:S(2)}, u32[]{:S(2)}) collective-permute-start(bf16[176,768]{1,0:T(8,128)(2,1)S(1)} %get-tuple-element.44), channel_id=1, source_target_pairs={{0,2},{1,3},{2,0},{3,1},{4,6},{5,7},{6,4},{7,5},{8,10},{9,11},{10,... | collective-permute-start | bytes 811016 | tf_op jit(solution)/shard_map/ppermute | solution.py:295
  38.7 7.9 %collective-permute-start.13 = (bf16[160,768]{1,0:T(8,128)(2,1)S(1)}, bf16[160,768]{1,0:T(8,128)(2,1)S(1)}, u32[]{:S(2)}, u32[]{:S(2)}) collective-permute-start(bf16[160,768]{1,0:T(8,128)(2,1)S(1)} %get-tuple-element.54), channel_id=1, source_target_pairs={{0,16},{16,0},{1,17},{17,1},{2,18},{18,2},{3,19},{19,3},{4,20},{20... | collective-permute-start | bytes 737288 | tf_op jit(solution)/shard_map/ppermute | solution.py:298
  40.7 12.0 %collective-permute-start.12 = (bf16[128,768]{1,0:T(8,128)(2,1)S(1)}, bf16[128,768]{1,0:T(8,128)(2,1)S(1)}, u32[]{:S(2)}, u32[]{:S(2)}) collective-permute-start(bf16[128,768]{1,0:T(8,128)(2,1)S(1)} %shard_map.101), channel_id=1, source_target_pairs={{0,12},{1,13},{2,14},{3,15},{4,8},{5,9},{6,10},{7,11},{8,4},{9,5},... | collective-permute-start | bytes 589832 | tf_op jit(solution)/shard_map/ppermute | solution.py:295
  44.6 10.3 %collective-permute-start.10 = (bf16[128,768]{1,0:T(8,128)(2,1)S(1)}, bf16[128,768]{1,0:T(8,128)(2,1)S(1)}, u32[]{:S(2)}, u32[]{:S(2)}) collective-permute-start(bf16[128,768]{1,0:T(8,128)(2,1)S(1)} %get-tuple-element.48), channel_id=1, source_target_pairs={{0,4},{1,5},{2,6},{3,7},{4,0},{5,1},{6,2},{7,3},{8,12},{9,13},{10,... | collective-permute-start | bytes 589832 | tf_op jit(solution)/shard_map/ppermute | solution.py:295
  44.6 16.1 %collective-permute-start.11 = (bf16[128,768]{1,0:T(8,128)(2,1)S(1)}, bf16[128,768]{1,0:T(8,128)(2,1)S(1)}, u32[]{:S(2)}, u32[]{:S(2)}) collective-permute-start(bf16[128,768]{1,0:T(8,128)(2,1)S(1)} %get-tuple-element.49), channel_id=1, source_target_pairs={{0,8},{1,9},{2,10},{3,11},{4,12},{5,13},{6,14},{7,15},{8,0},{9,1},... | collective-permute-start | bytes 589832 | tf_op jit(solution)/shard_map/ppermute | solution.py:295
  45.3 15.4 %collective-permute-start.9 = (bf16[176,768]{1,0:T(8,128)(2,1)S(1)}, bf16[176,768]{1,0:T(8,128)(2,1)S(1)}, u32[]{:S(2)}, u32[]{:S(2)}) collective-permute-start(bf16[176,768]{1,0:T(8,128)(2,1)S(1)} %shard_map.100.mine_ref), channel_id=1, source_target_pairs={{0,16},{16,0},{1,17},{17,1},{2,18},{18,2},{3,19},{19,3},{4,20},{20... | collective-permute-start | bytes 811016 | tf_op jit(solution)/shard_map/ppermute | solution.py:298
  46.7 4.9 %collective-permute-start.14 = (bf16[80,768]{1,0:T(8,128)(2,1)S(1)}, bf16[80,768]{1,0:T(8,128)(2,1)S(1)}, u32[]{:S(2)}, u32[]{:S(2)}) collective-permute-start(bf16[80,768]{1,0:T(8,128)(2,1)S(1)} %slice.12), channel_id=1, source_target_pairs={{0,2},{1,3},{2,0},{3,1},{4,6},{5,7},{6,4},{7,5},{8,10},{9,11},{10,... | collective-permute-start | bytes 368648 | tf_op jit(solution)/shard_map/ppermute | solution.py:295
